TPU v7x, 32 devices: a whole 2x2x4 slice. The times are simulated.
32 devices in a mesh: groups: 2 (over y), feat: 4 (over z), layer: 2 (over x), tok: 2 (over core).
Axes of the slice: x: 2, y: 2, z: 4, core: 2. Of those that a mesh axis runs over, the one named last changes fastest.
Arguments:
- residual_in: float32 [256, 2, 1792], P('groups', 'tok', 'feat'), parts along dimension 0, may hold values from -6 to 6
- attn_scale: float32 [2, 256], P('layer', 'groups'), parts along dimension 1, may hold values from 0.4 to 2.5
- mlp_scale: float32 [2, 256], P('layer', 'groups'), parts along dimension 1, may hold values from 0.4 to 2.5
- patterns: bfloat16 [2, 8, 4, 64, 64], P('layer', None, 'groups'), parts along dimension 2, may hold values from 0.0029907227 to 0.059814453
- lengths: int32 [4], P('groups'), parts along dimension 0, may hold values from 16 to 64
- value_proj: bfloat16 [2, 2, 1792, 1024], P('layer', 'tok', None, 'feat'), may hold values from -0.09375 to 0.09375
- out_proj: bfloat16 [2, 4, 256, 2, 2, 1792], P('layer', None, None, None, 'tok', 'feat'), may hold values from -0.125 to 0.125
- enc_weight: bfloat16 [2, 2, 1792, 512], P('layer', 'tok', None, 'feat'), may hold values from -0.09375 to 0.09375
- enc_bias: float32 [2, 512], P('layer', 'feat'), may hold values from -3 to 3
- dec_weight: bfloat16 [2, 2, 512, 2, 1792], P('layer', None, None, 'tok', 'feat'), may hold values from -0.25 to 0.25
- errors: float32 [2, 256, 2, 1792], P('layer', 'groups', 'tok', 'feat'), parts along dimension 1, may hold values from -4 to 4
- clamp_mode: int32 [2, 16384], P('layer', 'feat'), may hold values from 0 to 2
- clamp_index: int32 [2, 16384], P('layer', 'feat'), may hold values from 0 to 63
- clamp_values: float32 [64], replicated, may hold values from 0.25 to 3
- active_blocks: int32 [2, 4], P('layer', 'feat'), may hold values from 0 to 31
Outputs:
- residual_out: float32 [2, 256, 2, 1792], P('layer', 'groups', 'tok', 'feat'), parts along dimension 1
- features: bfloat16 [2, 256, 512], P('layer', 'groups', 'feat'), parts along dimension 1
There are 2 independent parts, one for each index of `groups`. A program takes and returns all parts, laid end to end along the dimension named above; an argument that names none is the same for every part. Nothing has to cross between parts.
Inputs may be any that keep to these rules, and one draw needn't show every extreme that they name: `clamp_mode`: 0 leaves a feature free, 1 sets it to its table value, 2 multiplies it by its table value. `lengths`: positions at or past a prompt's length are padding.
All inputs are finite; a program needn't handle non-finite values.
Results may differ from a plain program's by a relative error of at most 0.018.
Values may be sent and summed in bfloat16 or wider, within the bound.
A program may use at most 64 MiB of HBM per device.

v0:
```python
import functools

import jax
import jax.numpy as jnp
from jax import lax
from jax.experimental import pallas as pl
from jax.experimental.pallas import tpu as pltpu
from jax.sharding import PartitionSpec as P

F32 = jnp.float32
BF16 = jnp.bfloat16
NT = (((1,), (1,)), ((), ()))


def column(row):
    rows = row.shape[1]
    return jnp.transpose(jnp.broadcast_to(row, (128, rows)))[:, 0:1]


def kernel(
    sizes,
    lengths, table, chosen,
    scale_attn, scale_mlp, bias, mode_row, index_row,
    x_in, err_in, pat_in, wv_in, wo_in, we_in, wd_in,
    out_ref, feat_ref,
    x_t, err_t, pat, wv, wo, we, wd,
    xbuf, slots, vals, feats, part_v, part_v2, part_e, part_e2, e_out, e_in,
    next_scale, nbuf, xsend, acc_in, acc_out, att, err, wek, relay_in, relay_mid,
    local_sem, xs_send, xs_recv, ns_send, v_send, v_recv, m_send, m_recv, f_send, f_recv,
    t_send, t_recv, up_send, up_recv, one_send, one_recv, a_send, a_recv,
    w_send, w_recv, b_send, b_recv,
):
    layers, feat_n, seq, prompts, head_dim, per_group, kv, width, block, rows, entries, shares = sizes
    me_g = lax.axis_index("groups")
    me_l = lax.axis_index("layer")
    me_f = lax.axis_index("feat")
    me_t = lax.axis_index("tok")
    has_next = me_l < layers - 1
    has_prev = me_l > 0
    is_first = jnp.logical_not(has_prev)
    other = 1 - me_t
    nxt = jnp.minimum(me_l + 1, layers - 1)
    prv = jnp.maximum(me_l - 1, 0)
    streams = range(prompts)

    loads = [
        pltpu.make_async_copy(src, dst, local_sem.at[i])
        for i, (src, dst) in enumerate(
            ((x_in, x_t), (we_in, we), (wv_in, wv), (pat_in, pat), (wo_in, wo), (wd_in, wd), (err_in, err_t))
        )
    ]
    for load in loads:
        load.start()
    l_x, l_we, l_wv, l_pat, l_wo, l_wd, l_err = loads

    barrier = pltpu.get_barrier_semaphore()
    mesh_id = pl.DeviceIdType.MESH
    pl.semaphore_signal(barrier, inc=1, device_id={"tok": other}, device_id_type=mesh_id)
    for j in range(1, feat_n):
        pl.semaphore_signal(barrier, inc=1, device_id={"feat": (me_f + j) % feat_n}, device_id_type=mesh_id)

    @pl.when(has_next)
    def _():
        for s in range(feat_n):
            pl.semaphore_signal(barrier, inc=1, device_id={"layer": nxt, "feat": s}, device_id_type=mesh_id)

    @pl.when(has_prev)
    def _():
        for s in range(feat_n):
            pl.semaphore_signal(barrier, inc=1, device_id={"layer": prv, "feat": s}, device_id_type=mesh_id)

    def send(src, dst, ss, rs, where):
        return pltpu.make_async_remote_copy(
            src_ref=src, dst_ref=dst, send_sem=ss, recv_sem=rs, device_id=where, device_id_type=mesh_id
        )

    def peer(j):
        return (me_f + j) % feat_n

    def part(p):
        return pl.ds(p * seq, seq)

    l_x.wait()
    x_rows = jnp.transpose(x_t[...])
    normed = (x_rows * column(scale_attn[...])).astype(BF16)

    @pl.when(is_first)
    def _():
        for p in streams:
            slots[p, me_f] = normed[p * seq : (p + 1) * seq]
            xbuf[p] = x_rows[p * seq : (p + 1) * seq]

    for g in range(1, shares):
        @pl.when(is_first)
        def _():
            pl.semaphore_signal(
                barrier, inc=1, device_id={"groups": (me_g + g) % shares, "layer": nxt}, device_id_type=mesh_id
            )

        @pl.when(me_l == 1)
        def _():
            pl.semaphore_signal(
                barrier, inc=1, device_id={"groups": (me_g + g) % shares, "layer": prv}, device_id_type=mesh_id
            )

    extra = (shares - 1) * (1 - jnp.minimum(me_l // 2, 1))
    neighbours = 1 + jnp.minimum(me_l, 1) + jnp.minimum(layers - 1 - me_l, 1)
    pl.semaphore_wait(barrier, feat_n * neighbours + extra)

    def to_peers(ref, ss, rs, p):
        copies = [
            send(ref.at[p, me_f], ref.at[p, me_f], ss.at[p, j], rs.at[p, me_f], {"feat": peer(j)})
            for j in range(1, feat_n)
        ]
        for copy in copies:
            copy.start()
        return copies

    def arrived(ref, ss, rs, p, s):
        send(ref.at[p, s], ref.at[p, s], ss.at[p, 0], rs.at[p, s], {"tok": other}).wait_recv()

    def await_peer(ref, ss, rs, p, s):
        @pl.when(me_f != s)
        def _():
            arrived(ref, ss, rs, p, s)

    @pl.when(is_first)
    def _():
        for p in streams:
            to_peers(slots, xs_send, xs_recv, p)

    scale_up = send(scale_attn, next_scale, one_send.at[0], one_recv.at[0], {"layer": prv})
    x_up = [send(xsend.at[p], xbuf.at[p], up_send.at[p], up_recv.at[p], {"layer": nxt}) for p in streams]

    @pl.when(has_prev)
    def _():
        scale_up.start()

    def we_rows(s):
        return we.at[pl.ds(pl.multiple_of(s * width, 16), width)]

    l_we.wait()
    own_rows = pltpu.make_async_copy(we_rows(me_f), wek.at[me_f], local_sem.at[7])
    own_rows.start()
    share = width // shares
    my_share = me_g if shares > 1 else 0
    front = pl.ds(0, share)
    first_up = [
        send(
            we.at[pl.ds(pl.multiple_of(peer(j) * width + my_share * share, 16), share)],
            relay_in.at[peer(j), front], w_send.at[0, j], w_recv.at[0, peer(j)], {"layer": nxt},
        )
        for j in range(1, feat_n)
    ]
    across = [
        send(
            relay_in.at[peer(j), front], relay_mid.at[me_f, front],
            w_send.at[1, j], w_recv.at[1, me_f], {"feat": peer(j)},
        )
        for j in range(1, feat_n)
    ]
    back = [
        [
            send(
                relay_mid.at[peer(j), front],
                wek.at[peer(j), pl.ds(pl.multiple_of(my_share * share, 16), share)],
                b_send.at[g, j], b_recv.at[my_share, peer(j)],
                {"layer": prv, "groups": (me_g + g) % shares} if g else {"layer": prv},
            )
            for g in range(shares)
        ]
        for j in range(1, feat_n)
    ]
    direct = [
        send(we_rows(peer(j)), wek.at[me_f], w_send.at[3, j], w_recv.at[2, me_f], {"feat": peer(j)})
        for j in range(1, feat_n)
    ]

    def w_arrived(ref, stage, s):
        part_ref = ref.at[s, front] if stage < 2 else ref.at[s]
        send(part_ref, part_ref, w_send.at[stage, 0], w_recv.at[stage, s], {"tok": other}).wait_recv()

    @pl.when(is_first)
    def _():
        for copy in first_up:
            copy.start()

    @pl.when(me_l == 1)
    def _():
        for j in range(1, feat_n):
            w_arrived(relay_in, 0, peer(j))
            across[j - 1].start()
        for j in range(1, feat_n):
            w_arrived(relay_mid, 1, peer(j))
            for copy in back[j - 1]:
                copy.start()

    @pl.when(has_prev)
    def _():
        for copy in direct:
            copy.start()

    ids = lax.broadcasted_iota(jnp.int32, (seq, 1), 0)
    lives = [ids < lengths[p] for p in streams]
    which = jnp.zeros((1, block), jnp.int32) + chosen[0, 0]
    modes = picks = jnp.zeros((1, block), jnp.int32)
    for b in range(mode_row.shape[1] // block):
        here = which == b
        modes = jnp.where(here, mode_row[:, b * block : (b + 1) * block], modes)
        picks = jnp.where(here, index_row[:, b * block : (b + 1) * block], picks)
    levels = jnp.zeros((1, block), F32)
    for v in range(entries):
        levels = jnp.where(picks == v, table[v], levels)
    mlp_col = column(scale_mlp[...])
    shift = bias[...]
    l_err.wait()
    err[...] = jnp.transpose(err_t[...])
    l_wv.wait()
    l_pat.wait()
    l_wo.wait()
    l_wd.wait()
    own_rows.wait()

    tok_v = [send(part_v.at[p], part_v2.at[p], t_send.at[0, p], t_recv.at[0, p], {"tok": other}) for p in streams]
    tok_e = [send(part_e.at[p], part_e2.at[p], t_send.at[1, p], t_recv.at[1, p], {"tok": other}) for p in streams]
    pending = []
    for p in streams:
        total = jnp.zeros((seq, kv), F32)
        for s in range(feat_n):
            @pl.when(jnp.logical_or(has_prev, me_f != s))
            def _():
                arrived(slots, xs_send, xs_recv, p, s)

            total += jnp.dot(slots[p, s], wv[pl.ds(s * width, width), :], preferred_element_type=F32)
        part_v[p] = total
        tok_v[p].start()
        tok_v[p].wait_recv()
        vals[p, me_f] = (part_v[p] + part_v2[p]).astype(BF16)
        pending += to_peers(vals, v_send, v_recv, p)

    q_ids = lax.broadcasted_iota(jnp.int32, (seq, seq), 0)
    k_ids = lax.broadcasted_iota(jnp.int32, (seq, seq), 1)
    for p in streams:
        keep = jnp.logical_and(k_ids <= q_ids, k_ids < lengths[p])
        total = jnp.zeros((seq, width), F32)
        for s in range(feat_n):
            await_peer(vals, v_send, v_recv, p, s)
            group = s * kv // head_dim
            d0 = s * kv % head_dim
            for u in range(per_group):
                weights = jnp.where(keep, pat[group * per_group + u, p].astype(F32), 0.0).astype(BF16)
                head = jnp.dot(weights, vals[p, s], preferred_element_type=F32).astype(BF16)
                total += lax.dot_general(head, wo[group, u, :, pl.ds(d0, kv)], NT, preferred_element_type=F32)

        @pl.when(has_prev)
        def _():
            x_up[p].wait_recv()

        if p == 0:
            for s in range(feat_n):
                @pl.when(jnp.logical_and(has_prev, me_f != s))
                def _():
                    w_arrived(wek, 2, s)

                @pl.when(jnp.logical_and(is_first, me_f != s))
                def _():
                    for g in range(shares):
                        here = wek.at[s, pl.ds(g * share, share)]
                        send(here, here, b_send.at[0, 0], b_recv.at[g, s], {"tok": other}).wait_recv()

        middle = xbuf[p] + total
        normed_mlp = (middle * mlp_col[p * seq : (p + 1) * seq]).astype(BF16)
        for j in range(1, feat_n):
            e_out[p, j] = jnp.dot(normed_mlp, wek[peer(j)], preferred_element_type=F32).astype(BF16)
            copy = send(e_out.at[p, j], e_in.at[p, me_f], m_send.at[p, j], m_recv.at[p, me_f], {"feat": peer(j)})
            copy.start()
            pending.append(copy)
        part_e[p] = jnp.dot(normed_mlp, wek[me_f], preferred_element_type=F32)
        att[part(p), :] = middle + err[part(p), :]

    for p in streams:
        for s in range(feat_n):
            @pl.when(me_f != s)
            def _():
                arrived(e_in, m_send, m_recv, p, s)
                part_e[p] += e_in[p, s].astype(F32)

        tok_e[p].start()
        tok_e[p].wait_recv()
        preact = part_e[p] + part_e2[p] + shift
        active = jnp.maximum(preact, 0.0)
        clamped = jnp.where(modes == 1, levels, jnp.where(modes == 2, active * levels, active))
        new_feats = jnp.where(lives[p], clamped, 0.0).astype(BF16)
        feats[p, me_f] = new_feats
        pending += to_peers(feats, f_send, f_recv, p)
        feat_ref[part(p), :] = new_feats

    def acc_copy(p, t):
        return send(acc_out.at[p, t], acc_in.at[p, t], a_send.at[p, t], a_recv.at[p, t], {"layer": nxt})

    def norm_up(p, s):
        return send(nbuf.at[p], slots.at[p, me_f], ns_send.at[p, s], xs_recv.at[p, me_f], {"layer": nxt, "feat": s})

    @pl.when(has_next)
    def _():
        send(scale_attn, next_scale, one_send.at[0], one_recv.at[0], {"layer": nxt}).wait_recv()

    for p in streams:
        @pl.when(has_prev)
        def _():
            for t in range(1, layers):
                @pl.when(t >= me_l)
                def _():
                    acc_copy(p, t).wait_recv()
            att[part(p), :] += acc_in[p, me_l]

        total = att[part(p), :]
        for s in range(feat_n):
            await_peer(feats, f_send, f_recv, p, s)
            total += lax.dot_general(feats[p, s], wd[me_l, :, pl.ds(s * block, block)], NT, preferred_element_type=F32)
        att[part(p), :] = total

        @pl.when(has_next)
        def _():
            after = att[part(p), :]
            nbuf[p] = (after * column(next_scale[...])[p * seq : (p + 1) * seq]).astype(BF16)
            for s in range(feat_n):
                norm_up(p, s).start()
            xsend[p] = after

    @pl.when(has_next)
    def _():
        for p in streams:
            x_up[p].start()
        for p in streams:
            for t in range(1, layers):
                @pl.when(t > me_l)
                def _():
                    total = jnp.zeros((seq, width), F32)
                    for s in range(feat_n):
                        total += lax.dot_general(
                            feats[p, s], wd[t, :, pl.ds(s * block, block)], NT, preferred_element_type=F32
                        )
                    acc_out[p, t] = total

                    @pl.when(has_prev)
                    def _():
                        acc_out[p, t] += acc_in[p, t]

                    acc_copy(p, t).start()

    out_ref[...] = jnp.transpose(att[...])

    @pl.when(is_first)
    def _():
        for p in streams:
            for j in range(1, feat_n):
                send(
                    slots.at[p, me_f], slots.at[p, me_f], xs_send.at[p, j], xs_recv.at[p, me_f], {"tok": other}
                ).wait_send()
        for copy in first_up:
            copy.wait_send()

    @pl.when(me_l == 1)
    def _():
        for copy in sum(back, across):
            copy.wait_send()

    @pl.when(has_prev)
    def _():
        scale_up.wait_send()
        for copy in direct:
            copy.wait_send()

    for copy in tok_v + tok_e + pending:
        copy.wait_send()

    @pl.when(has_next)
    def _():
        for p in streams:
            for s in range(feat_n):
                norm_up(p, s).wait_send()
            x_up[p].wait_send()
            for t in range(1, layers):
                @pl.when(t > me_l)
                def _():
                    acc_copy(p, t).wait_send()


def store(x_ref, f_ref, out_ref, feat_ref, sems):
    copies = [
        pltpu.make_async_copy(x_ref, out_ref, sems.at[0]),
        pltpu.make_async_copy(f_ref, feat_ref, sems.at[1]),
    ]
    for copy in copies:
        copy.start()
    for copy in copies:
        copy.wait()


def local(
    residual_in, attn_scale, mlp_scale, patterns, lengths, value_proj, out_proj, enc_weight, enc_bias,
    dec_weight, errors, clamp_mode, clamp_index, clamp_values, active_blocks,
):
    layers = lax.axis_size("layer")
    feat_n = lax.axis_size("feat")
    prompts, seq = patterns.shape[2], patterns.shape[3]
    head_dim, per_group = out_proj.shape[2], out_proj.shape[3]
    kv = value_proj.shape[3]
    rows, _, width = residual_in.shape
    block = enc_bias.shape[1]
    entries = clamp_values.shape[0]
    groups = lax.axis_size("groups")
    shares = groups if width % (16 * groups) == 0 else 1
    sizes = (layers, feat_n, seq, prompts, head_dim, per_group, kv, width, block, rows, entries, shares)
    x_in = residual_in[:, 0, :].T
    err_in = errors[0, :, 0, :].T
    pat_in = patterns[0]
    wv_in = value_proj[0, 0]
    wo_in = jnp.transpose(out_proj[0, :, :, :, 0, :], (0, 2, 3, 1))
    we_in = enc_weight[0, 0]
    wd_in = jnp.transpose(dec_weight[0, :, :, 0, :], (0, 2, 1))
    smem = pl.BlockSpec(memory_space=pltpu.SMEM)
    vmem = pl.BlockSpec(memory_space=pltpu.VMEM)
    hbm = pl.BlockSpec(memory_space=pl.ANY)
    big = (x_in, err_in, pat_in, wv_in, wo_in, we_in, wd_in)
    dma = pltpu.SemaphoreType.DMA
    out_t, out_f = pl.pallas_call(
        functools.partial(kernel, sizes),
        out_shape=(
            jax.ShapeDtypeStruct((width, rows), F32),
            jax.ShapeDtypeStruct((rows, block), BF16),
        ),
        in_specs=[smem] * 3 + [vmem] * 5 + [hbm] * 7,
        out_specs=(vmem, vmem),
        scratch_shapes=[pltpu.VMEM(a.shape, a.dtype) for a in big]
        + [
            pltpu.VMEM((prompts, seq, width), F32),
            pltpu.VMEM((prompts, feat_n, seq, width), BF16),
            pltpu.VMEM((prompts, feat_n, seq, kv), BF16),
            pltpu.VMEM((prompts, feat_n, seq, block), BF16),
            pltpu.VMEM((prompts, seq, kv), F32),
            pltpu.VMEM((prompts, seq, kv), F32),
            pltpu.VMEM((prompts, seq, block), F32),
            pltpu.VMEM((prompts, seq, block), F32),
            pltpu.VMEM((prompts, feat_n, seq, block), BF16),
            pltpu.VMEM((prompts, feat_n, seq, block), BF16),
            pltpu.VMEM((1, rows), F32),
            pltpu.VMEM((prompts, seq, width), BF16),
            pltpu.VMEM((prompts, seq, width), F32),
            pltpu.VMEM((prompts, layers, seq, width), F32),
            pltpu.VMEM((prompts, layers, seq, width), F32),
            pltpu.VMEM((rows, width), F32),
            pltpu.VMEM((rows, width), F32),
        ]
        + [pltpu.VMEM((feat_n, width, block), BF16)] * 3
        + [dma((8,))]
        + [dma((prompts, feat_n))] * 9
        + [dma((2, prompts))] * 2
        + [dma((prompts,))] * 2
        + [dma((1,))] * 2
        + [dma((prompts, layers))] * 2
        + [dma((4, feat_n)), dma((3, feat_n))]
        + [dma((shares, feat_n))] * 2,
        compiler_params=pltpu.CompilerParams(collective_id=0, has_side_effects=True),
    )(lengths, clamp_values, active_blocks, attn_scale, mlp_scale, enc_bias, clamp_mode, clamp_index, *big)
    out_t, out_f = pl.pallas_call(
        store,
        out_shape=(
            jax.ShapeDtypeStruct((width, rows), F32),
            jax.ShapeDtypeStruct((rows, block), BF16),
        ),
        in_specs=[vmem, vmem],
        out_specs=(hbm, hbm),
        scratch_shapes=[dma((2,))],
    )(out_t, out_f)
    return out_t.T[None, :, None, :], out_f[None]


def solution(mesh):
    return jax.shard_map(
        local,
        mesh=mesh,
        in_specs=(
            P("groups", "tok", "feat"),
            P("layer", "groups"),
            P("layer", "groups"),
            P("layer", None, "groups", None, None),
            P("groups"),
            P("layer", "tok", None, "feat"),
            P("layer", None, None, None, "tok", "feat"),
            P("layer", "tok", None, "feat"),
            P("layer", "feat"),
            P("layer", None, None, "tok", "feat"),
            P("layer", "groups", "tok", "feat"),
            P("layer", "feat"),
            P("layer", "feat"),
            P(),
            P("layer", "feat"),
        ),
        out_specs=(P("layer", "groups", "tok", "feat"), P("layer", "groups", "feat")),
        check_vma=False,
    )
```

profile of v0, /device:TPU:7, one launch (start us, length us, event | category | flops | bytes accessed | tf_op | source)
XLA Modules:
  0.0 67.7 jit_solution(8917957831525773713)
XLA Ops:
  1.3 64.8 %shard_map.158 = (f32[448,128]{1,0:T(8,128)}, bf16[128,128]{1,0:T(8,128)(2,1)}) custom-call(s32[2]{0:T(128)} %lengths.1, f32[64]{0:T(128)} %table.1, s32[1,1]{1,0:T(1,128)S(6)} %copy.17.chosen, f32[1,128]{1,0:T(1,128)} %scale_attn.1, f32[1,128]{1,0:T(1,128)} %scale_mlp.1, f32[1,128]{1,0:T(1,128)} %bias.1, s32[1,4096]{1,0:T(1,128)} %mode_row.1, ...), custom_call_target="tpu_custom_call" | custom-call | tf_op jit(solution)/shard_map/pallas_call | solution.py:428
  66.1 1.6 %shard_map.159 = (f32[448,128]{1,0:T(8,128)}, bf16[128,128]{1,0:T(8,128)(2,1)}) custom-call(f32[448,128]{1,0:T(8,128)} %get-tuple-element.6.x_ref, bf16[128,128]{1,0:T(8,128)(2,1)} %get-tuple-element.7.f_ref), custom_call_target="tpu_custom_call" | custom-call | tf_op jit(solution)/shard_map/pallas_call | solution.py:467
where the time goes:
time: 67.9 us; the launch traced here: 67.7 us
  Pallas kernels  66.4 us (98%)
  between operations  1.29 us (2%)
    pallas_call x1, Pallas kernels, local(): pl.pallas_call(functools.partial(kernel, sizes), out_shape=(jax.ShapeDtyp...  64.8 us
    pallas_call x1, Pallas kernels, local(): pl.pallas_call(store, out_shape=(jax.ShapeDtypeStruct((width, rows), F32)...  1.65 us

commit v1 on v0

v1 whole, which is shorter than its diff:
```python
import functools

import jax
import jax.numpy as jnp
from jax import lax
from jax.experimental import pallas as pl
from jax.experimental.pallas import tpu as pltpu
from jax.sharding import PartitionSpec as P

F32 = jnp.float32
BF16 = jnp.bfloat16
NT = (((1,), (1,)), ((), ()))


def column(row):
    rows = row.shape[1]
    return jnp.transpose(jnp.broadcast_to(row, (128, rows)))[:, 0:1]


def kernel(
    sizes,
    lengths_in, table_in, chosen_in, attn_in, mlp_in, bias_in, mode_in, index_in,
    x_in, err_in, pat_in, wv_in, wo_in, we_in, wd_in,
    out_ref, feat_ref,
    lengths, table, chosen, scale_attn, scale_mlp, bias, mode_row, index_row,
    x_t, err_t, pat, wv, wo, we, wd,
    xbuf, slots, relay_x, nbuf, masked, part_v, part_v2, vals, part_e, e_out, e_in, feats,
    acc_in, acc_out, att, err, wek, relay_in, relay_mid,
    local_sem, xs_send, xs_recv, rx_send, ns_send, zx_send, zx_recv, zf_send, t_send, t_recv,
    v_send, v_recv, vf_send, m_send, m_recv, f_send, f_recv, a_send, a_recv,
    w_send, w_recv, b_send, b_recv,
):
    layers, feat_n, seq, prompts, head_dim, per_group, kv, width, block, rows, entries, shares = sizes
    half = seq // 2
    me_g = lax.axis_index("groups")
    me_l = lax.axis_index("layer")
    me_f = lax.axis_index("feat")
    me_t = lax.axis_index("tok")
    has_next = me_l < layers - 1
    has_prev = me_l > 0
    is_first = jnp.logical_not(has_prev)
    other = 1 - me_t
    nxt = jnp.minimum(me_l + 1, layers - 1)
    prv = jnp.maximum(me_l - 1, 0)
    streams = range(prompts)
    ends = (0, feat_n - 1)
    at_end = jnp.logical_or(me_f == 0, me_f == feat_n - 1)
    order = sorted(range(feat_n), key=lambda s: abs(2 * s - feat_n + 1))
    low_side = 2 * me_f < feat_n
    both = jnp.logical_and

    loads = [
        pltpu.make_async_copy(src, dst, local_sem.at[i])
        for i, (src, dst) in enumerate(
            (
                (x_in, x_t), (we_in, we), (attn_in, scale_attn), (lengths_in, lengths), (table_in, table),
                (chosen_in, chosen), (mlp_in, scale_mlp), (bias_in, bias), (mode_in, mode_row),
                (index_in, index_row), (wv_in, wv), (pat_in, pat), (wo_in, wo), (wd_in, wd), (err_in, err_t),
            )
        )
    ]
    for load in loads:
        load.start()
    l_x, l_we = loads[:2]

    barrier = pltpu.get_barrier_semaphore()
    mesh_id = pl.DeviceIdType.MESH

    def greet(where):
        pl.semaphore_signal(barrier, inc=1, device_id=where, device_id_type=mesh_id)

    for j in range(1, feat_n):
        for t in range(2):
            greet({"feat": (me_f + j) % feat_n, "tok": t})
    pl.when(has_next)(lambda: greet({"layer": nxt}))
    pl.when(has_prev)(lambda: greet({"layer": prv}))
    for g in range(1, shares):
        pl.when(is_first)(lambda: greet({"groups": (me_g + g) % shares, "layer": nxt}))
        pl.when(me_l == 1)(lambda: greet({"groups": (me_g + g) % shares, "layer": prv}))
    greet({"tok": other})

    def send(src, dst, ss, rs, where):
        return pltpu.make_async_remote_copy(
            src_ref=src, dst_ref=dst, send_sem=ss, recv_sem=rs, device_id=where, device_id_type=mesh_id
        )

    def peer(j):
        return (me_f + j) % feat_n

    def far(k):
        down = feat_n - 1 - k
        return jnp.where(low_side, down - jnp.where(down <= me_f, 1, 0), k + jnp.where(k >= me_f, 1, 0))

    def part(p):
        return pl.ds(p * seq, seq)

    pending = []

    def launch(copy, cond=None):
        pending.append((copy, cond))
        if cond is None:
            copy.start()
        else:
            pl.when(cond)(copy.start)

    def landed(ref, ss, rs):
        send(ref, ref, ss, rs, {"tok": other}).wait_recv()

    l_x.wait()
    x_rows = jnp.transpose(x_t[...])

    @pl.when(is_first)
    def _():
        x_half = x_rows.astype(BF16)
        for p in streams:
            slots[p, me_f] = x_half[p * seq : (p + 1) * seq]
            xbuf[p] = x_rows[p * seq : (p + 1) * seq]

    extra = (shares - 1) * (1 - jnp.minimum(me_l // 2, 1))
    pl.semaphore_wait(
        barrier, 2 * feat_n - 1 + jnp.minimum(me_l, 1) + jnp.minimum(layers - 1 - me_l, 1) + extra
    )

    def share_x(p, step, cond):
        to = me_f + step
        cond = both(both(to >= 0, to < feat_n), cond)
        to = jnp.clip(to, 0, feat_n - 1)
        slot = slots.at[p, me_f]
        launch(send(slot, slot, xs_send.at[p, to], xs_recv.at[p, me_f], {"feat": to}), cond)

    def x_landed(p, s):
        landed(slots.at[p, s], xs_send.at[p, 0], xs_recv.at[p, s])

    for p in streams:
        for step in (2, -2, 1, -1):
            share_x(p, step, is_first)

    def we_rows(s):
        return we.at[pl.ds(pl.multiple_of(s * width, 16), width)]

    l_we.wait()
    own_rows = pltpu.make_async_copy(we_rows(me_f), wek.at[me_f], local_sem.at[len(loads)])
    own_rows.start()
    share = width // shares
    my_share = me_g if shares > 1 else 0
    front = pl.ds(0, share)
    first_up = [
        send(
            we.at[pl.ds(pl.multiple_of(peer(j) * width + my_share * share, 16), share)],
            relay_in.at[peer(j), front], w_send.at[0, j], w_recv.at[0, peer(j)], {"layer": nxt},
        )
        for j in range(1, feat_n)
    ]
    across = [
        send(
            relay_in.at[peer(j), front], relay_mid.at[me_f, front],
            w_send.at[1, j], w_recv.at[1, me_f], {"feat": peer(j)},
        )
        for j in range(1, feat_n)
    ]
    back = [
        [
            send(
                relay_mid.at[peer(j), front],
                wek.at[peer(j), pl.ds(pl.multiple_of(my_share * share, 16), share)],
                b_send.at[g, j], b_recv.at[my_share, peer(j)],
                {"layer": prv, "groups": (me_g + g) % shares} if g else {"layer": prv},
            )
            for g in range(shares)
        ]
        for j in range(1, feat_n)
    ]
    direct = [
        send(we_rows(peer(j)), wek.at[me_f], w_send.at[3, j], w_recv.at[2, me_f], {"feat": peer(j)})
        for j in range(1, feat_n)
    ]

    def w_arrived(ref, stage, s):
        part_ref = ref.at[s, front] if stage < 2 else ref.at[s]
        send(part_ref, part_ref, w_send.at[stage, 0], w_recv.at[stage, s], {"tok": other}).wait_recv()

    @pl.when(is_first)
    def _():
        for copy in first_up:
            copy.start()

    @pl.when(me_l == 1)
    def _():
        for j in range(1, feat_n):
            w_arrived(relay_in, 0, peer(j))
            across[j - 1].start()
        for j in range(1, feat_n):
            w_arrived(relay_mid, 1, peer(j))
            for copy in back[j - 1]:
                copy.start()

    @pl.when(has_prev)
    def _():
        for copy in direct:
            copy.start()

    for load in loads[2:]:
        load.wait()
    ids = lax.broadcasted_iota(jnp.int32, (half, 1), 0) + me_t * half
    lives = [ids < lengths[p] for p in streams]
    which = jnp.zeros((1, block), jnp.int32) + chosen[0, 0]
    modes = picks = jnp.zeros((1, block), jnp.int32)
    for b in range(mode_row.shape[1] // block):
        here = which == b
        modes = jnp.where(here, mode_row[:, b * block : (b + 1) * block], modes)
        picks = jnp.where(here, index_row[:, b * block : (b + 1) * block], picks)
    levels = jnp.zeros((1, block), F32)
    for v in range(entries):
        levels = jnp.where(picks == v, table[v], levels)
    attn_col = column(scale_attn[...])
    mlp_col = column(scale_mlp[...])
    shift = bias[...]
    err[...] = jnp.transpose(err_t[...])
    q_ids = lax.broadcasted_iota(jnp.int32, (seq, seq), 0)
    k_ids = lax.broadcasted_iota(jnp.int32, (seq, seq), 1)
    for p in streams:
        keep = both(k_ids <= q_ids, k_ids < lengths[p])
        for h in range(pat.shape[0]):
            masked[h // per_group, p, pl.ds(h % per_group * seq, seq), :] = jnp.where(
                keep, pat[h, p].astype(F32), 0.0
            ).astype(BF16)
        e_in[p, me_f, me_t] = jnp.zeros((half, block), BF16)
    own_rows.wait()

    for p in streams:
        @pl.when(has_prev)
        def _():
            x_landed(p, me_f)
            xbuf[p] = slots[p, me_f].astype(F32)

        for k in range(1, feat_n):
            for step in (feat_n - k, k - feat_n):
                share_x(p, step, has_prev if abs(step) == 1 else both(has_prev, jnp.logical_not(at_end)))

    for p in streams:
        total = jnp.zeros((seq, kv), F32)
        for s in order:
            pl.when(me_f != s)(lambda: x_landed(p, s))
            for side, step in enumerate((1, -1)):
                to = me_f + step
                inside = both(to >= 0, to < feat_n)
                if_far = (to - s) * step > 2
                launch(
                    send(
                        slots.at[p, s], slots.at[p, s], rx_send.at[p, s, side], xs_recv.at[p, s],
                        {"feat": jnp.clip(to, 0, feat_n - 1)},
                    ),
                    both(is_first, both(inside, if_far)),
                )
            total += jnp.dot(slots[p, s], wv[pl.ds(s * width, width), :], preferred_element_type=F32)
        total *= attn_col[p * seq : (p + 1) * seq]
        part_v[p] = total.reshape(2, half, kv)
        launch(send(part_v.at[p, other], part_v2.at[p], t_send.at[p], t_recv.at[p], {"tok": other}))
        landed(part_v2.at[p], t_send.at[p], t_recv.at[p])
        vals[p, me_f, me_t] = (part_v[p, me_t] + part_v2[p]).astype(BF16)
        mine = vals.at[p, me_f, me_t]
        for k in range(feat_n - 1):
            launch(send(mine, mine, v_send.at[p, k], v_recv.at[p, me_f, me_t], {"feat": far(k)}))
        launch(send(mine, mine, vf_send.at[p, me_f], v_recv.at[p, me_f, me_t], {"tok": other}))

    def take(p, s):
        got = vals.at[p, s, me_t]

        @pl.when(me_f != s)
        def _():
            landed(got, vf_send.at[p, s], v_recv.at[p, s, me_t])
            send(got, got, vf_send.at[p, s], v_recv.at[p, s, me_t], {"tok": other}).start()

        pending.append((send(got, got, vf_send.at[p, s], v_recv.at[p, s, me_t], {"tok": other}), me_f != s))

    for p in streams:
        total = jnp.zeros((seq, width), F32)
        for n in range(feat_n + 1):
            if n < feat_n:
                take(p, order[n])
            if n == 0:
                continue
            s = order[n - 1]
            landed(vals.at[p, s, other], vf_send.at[p, s], v_recv.at[p, s, other])
            group = s * kv // head_dim
            d0 = s * kv % head_dim
            heads = jnp.dot(masked[group, p], vals[p, s].reshape(seq, kv), preferred_element_type=F32).astype(BF16)
            for u in range(per_group):
                total += lax.dot_general(
                    heads[u * seq : (u + 1) * seq], wo[group, u, :, pl.ds(d0, kv)], NT, preferred_element_type=F32
                )

        if p == 0:
            for s in range(feat_n):
                @pl.when(both(has_prev, me_f != s))
                def _():
                    w_arrived(wek, 2, s)

                @pl.when(both(is_first, me_f != s))
                def _():
                    for g in range(shares):
                        here = wek.at[s, pl.ds(g * share, share)]
                        send(here, here, b_send.at[0, 0], b_recv.at[g, s], {"tok": other}).wait_recv()

        middle = xbuf[p] + total
        normed_mlp = (middle * mlp_col[p * seq : (p + 1) * seq]).astype(BF16)
        for k in range(feat_n):
            to = far(k) if k < feat_n - 1 else me_f
            result = jnp.dot(normed_mlp, wek[to], preferred_element_type=F32).reshape(2, half, block)
            e_out[p, k] = result.astype(BF16)
            if k < feat_n - 1:
                for t in range(2):
                    launch(
                        send(
                            e_out.at[p, k, t], e_in.at[p, me_f, me_t], m_send.at[p, k, t],
                            m_recv.at[p, me_f, me_t], {"feat": to, "tok": t},
                        )
                    )
            else:
                part_e[p] = result
                launch(
                    send(
                        e_out.at[p, k, other], e_in.at[p, me_f, me_t], m_send.at[p, k, 0],
                        m_recv.at[p, me_f, me_t], {"tok": other},
                    )
                )
        att[part(p), :] = middle + err[part(p), :]

    def await_others(ref, ss, rs, p, s):
        for t in range(2):
            pl.when(jnp.logical_or(me_f != s, me_t != t))(
                lambda: landed(ref.at[p, s, t], ss.at[p, 0, 0], rs.at[p, s, t])
            )

    for p in streams:
        for s in order:
            await_others(e_in, m_send, m_recv, p, s)
        preact = part_e[p, me_t] + shift
        for s in range(feat_n):
            for t in range(2):
                preact += e_in[p, s, t].astype(F32)
        active = jnp.maximum(preact, 0.0)
        clamped = jnp.where(modes == 1, levels, jnp.where(modes == 2, active * levels, active))
        feats[p, me_f, me_t] = jnp.where(lives[p], clamped, 0.0).astype(BF16)
        mine = feats.at[p, me_f, me_t]
        for k in range(feat_n - 1):
            for t in range(2):
                launch(
                    send(mine, mine, f_send.at[p, k, t], f_recv.at[p, me_f, me_t], {"feat": far(k), "tok": t})
                )
        launch(send(mine, mine, f_send.at[p, feat_n - 1, 0], f_recv.at[p, me_f, me_t], {"tok": other}))

    def acc_copy(p, t):
        return send(acc_out.at[p, t], acc_in.at[p, t], a_send.at[p, t], a_recv.at[p, t], {"layer": nxt})

    for p in streams:
        @pl.when(has_prev)
        def _():
            for t in range(1, layers):
                @pl.when(t >= me_l)
                def _():
                    acc_copy(p, t).wait_recv()
            att[part(p), :] += acc_in[p, me_l]

        total = att[part(p), :]
        for s in order:
            await_others(feats, f_send, f_recv, p, s)
            total += lax.dot_general(
                feats[p, s].reshape(seq, block), wd[me_l, :, pl.ds(s * block, block)], NT,
                preferred_element_type=F32,
            )
        att[part(p), :] = total
        feat_ref[part(p), :] = feats[p, me_f].reshape(seq, block)

        @pl.when(has_next)
        def _():
            nbuf[p] = att[part(p), :].astype(BF16)

        for k in range(feat_n - 2):
            to = jnp.where(me_f == 0, feat_n - 1 - k, k)
            launch(
                send(
                    nbuf.at[p], relay_x.at[p, jnp.minimum(me_f, 1)], zx_send.at[p, k],
                    zx_recv.at[p, jnp.minimum(me_f, 1)], {"feat": to},
                ),
                both(has_next, at_end),
            )
        launch(send(nbuf.at[p], slots.at[p, me_f], ns_send.at[p], xs_recv.at[p, me_f], {"layer": nxt}), has_next)

    for p in streams:
        for e, src in enumerate(ends):
            relays = both(has_next, jnp.abs(me_f - src) > 1)
            pl.when(relays)(lambda: landed(relay_x.at[p, e], zx_send.at[p, 0], zx_recv.at[p, e]))
            launch(
                send(relay_x.at[p, e], slots.at[p, src], zf_send.at[p, e], xs_recv.at[p, src], {"layer": nxt}),
                relays,
            )

    @pl.when(has_next)
    def _():
        for p in streams:
            for t in range(1, layers):
                @pl.when(t > me_l)
                def _():
                    rest = att[part(p), :] - nbuf[p].astype(F32)
                    total = jnp.where(me_l + 1 == t, rest, 0.0)
                    for s in range(feat_n):
                        total += lax.dot_general(
                            feats[p, s].reshape(seq, block), wd[t, :, pl.ds(s * block, block)], NT,
                            preferred_element_type=F32,
                        )
                    acc_out[p, t] = total

                    @pl.when(has_prev)
                    def _():
                        acc_out[p, t] += acc_in[p, t]

                    acc_copy(p, t).start()

    out_ref[...] = jnp.transpose(att[...])

    @pl.when(is_first)
    def _():
        for copy in first_up:
            copy.wait_send()

    @pl.when(me_l == 1)
    def _():
        for copy in sum(back, across):
            copy.wait_send()

    @pl.when(has_prev)
    def _():
        for copy in direct:
            copy.wait_send()

    for copy, cond in pending:
        if cond is None:
            copy.wait_send()
        else:
            pl.when(cond)(copy.wait_send)

    @pl.when(has_next)
    def _():
        for p in streams:
            for t in range(1, layers):
                @pl.when(t > me_l)
                def _():
                    acc_copy(p, t).wait_send()


def store(x_ref, f_ref, out_ref, feat_ref, sems):
    copies = [
        pltpu.make_async_copy(x_ref, out_ref, sems.at[0]),
        pltpu.make_async_copy(f_ref, feat_ref, sems.at[1]),
    ]
    for copy in copies:
        copy.start()
    for copy in copies:
        copy.wait()


def local(
    residual_in, attn_scale, mlp_scale, patterns, lengths, value_proj, out_proj, enc_weight, enc_bias,
    dec_weight, errors, clamp_mode, clamp_index, clamp_values, active_blocks,
):
    layers = lax.axis_size("layer")
    feat_n = lax.axis_size("feat")
    prompts, seq = patterns.shape[2], patterns.shape[3]
    head_dim, per_group = out_proj.shape[2], out_proj.shape[3]
    kv = value_proj.shape[3]
    rows, _, width = residual_in.shape
    block = enc_bias.shape[1]
    entries = clamp_values.shape[0]
    groups = lax.axis_size("groups")
    shares = groups if width % (16 * groups) == 0 else 1
    sizes = (layers, feat_n, seq, prompts, head_dim, per_group, kv, width, block, rows, entries, shares)
    x_in = residual_in[:, 0, :].T
    err_in = errors[0, :, 0, :].T
    pat_in = patterns[0]
    wv_in = value_proj[0, 0]
    wo_in = jnp.transpose(out_proj[0, :, :, :, 0, :], (0, 2, 3, 1))
    we_in = enc_weight[0, 0]
    wd_in = jnp.transpose(dec_weight[0, :, :, 0, :], (0, 2, 1))
    smem = pltpu.SMEM
    vmem = pl.BlockSpec(memory_space=pltpu.VMEM)
    hbm = pl.BlockSpec(memory_space=pl.ANY)
    small = (lengths, clamp_values, active_blocks, attn_scale, mlp_scale, enc_bias, clamp_mode, clamp_index)
    big = (x_in, err_in, pat_in, wv_in, wo_in, we_in, wd_in)
    half = seq // 2
    kv_heads = out_proj.shape[1]
    dma = pltpu.SemaphoreType.DMA
    out_t, out_f = pl.pallas_call(
        functools.partial(kernel, sizes),
        out_shape=(pltpu.VMEM((width, rows), F32), pltpu.VMEM((rows, block), BF16)),
        in_specs=[hbm] * 15,
        out_specs=(vmem, vmem),
        scratch_shapes=[(smem if i < 3 else pltpu.VMEM)(a.shape, a.dtype) for i, a in enumerate(small)]
        + [pltpu.VMEM(a.shape, a.dtype) for a in big]
        + [
            pltpu.VMEM((prompts, seq, width), F32),
            pltpu.VMEM((prompts, feat_n, seq, width), BF16),
            pltpu.VMEM((prompts, 2, seq, width), BF16),
            pltpu.VMEM((prompts, seq, width), BF16),
            pltpu.VMEM((kv_heads, prompts, per_group * seq, seq), BF16),
            pltpu.VMEM((prompts, 2, half, kv), F32),
            pltpu.VMEM((prompts, half, kv), F32),
            pltpu.VMEM((prompts, feat_n, 2, half, kv), BF16),
            pltpu.VMEM((prompts, 2, half, block), F32),
            pltpu.VMEM((prompts, feat_n, 2, half, block), BF16),
            pltpu.VMEM((prompts, feat_n, 2, half, block), BF16),
            pltpu.VMEM((prompts, feat_n, 2, half, block), BF16),
            pltpu.VMEM((prompts, layers, seq, width), F32),
            pltpu.VMEM((prompts, layers, seq, width), F32),
            pltpu.VMEM((rows, width), F32),
            pltpu.VMEM((rows, width), F32),
        ]
        + [pltpu.VMEM((feat_n, width, block), BF16)] * 3
        + [dma((16,))]
        + [dma((prompts, feat_n))] * 2
        + [dma((prompts, feat_n, 2)), dma((prompts,)), dma((prompts, feat_n)), dma((prompts, 2)), dma((prompts, 2))]
        + [dma((prompts,))] * 2
        + [dma((prompts, feat_n)), dma((prompts, feat_n, 2)), dma((prompts, feat_n))]
        + [dma((prompts, feat_n, 2))] * 4
        + [dma((prompts, layers))] * 2
        + [dma((4, feat_n)), dma((3, feat_n))]
        + [dma((shares, feat_n))] * 2,
        compiler_params=pltpu.CompilerParams(collective_id=0, has_side_effects=True),
    )(*small, *big)
    out_t, out_f = pl.pallas_call(
        store,
        out_shape=(
            jax.ShapeDtypeStruct((width, rows), F32),
            jax.ShapeDtypeStruct((rows, block), BF16),
        ),
        in_specs=[vmem, vmem],
        out_specs=(hbm, hbm),
        scratch_shapes=[dma((2,))],
    )(out_t, out_f)
    return out_t.T[None, :, None, :], out_f[None]


def solution(mesh):
    return jax.shard_map(
        local,
        mesh=mesh,
        in_specs=(
            P("groups", "tok", "feat"),
            P("layer", "groups"),
            P("layer", "groups"),
            P("layer", None, "groups", None, None),
            P("groups"),
            P("layer", "tok", None, "feat"),
            P("layer", None, None, None, "tok", "feat"),
            P("layer", "tok", None, "feat"),
            P("layer", "feat"),
            P("layer", None, None, "tok", "feat"),
            P("layer", "groups", "tok", "feat"),
            P("layer", "feat"),
            P("layer", "feat"),
            P(),
            P("layer", "feat"),
        ),
        out_specs=(P("layer", "groups", "tok", "feat"), P("layer", "groups", "feat")),
        check_vma=False,
    )
```

time: 67.9 us -> 64 us (0.943)
  Pallas kernels: 66.4 us -> 61.1 us
  local copies, waits for them, and re-layouts: 0 us -> 1.27 us
    pallas_call x1, Pallas kernels: 64.8 us -> 59.5 us  [local(): pl.pallas_call(functools.partial(kernel, sizes), out_shape=(pltpu.VMEM((w...]
    unnamed x0 -> x4, local copies, waits for them, and re-layouts: none -> 1.27 us
where the time goes in v1:
time: 64 us; the launch traced here: 63.7 us
  Pallas kernels  61.1 us (95%)
  between operations  1.3 us (2%)
  local copies, waits for them, and re-layouts  1.27 us (2%)
    pallas_call x1, Pallas kernels, local(): pl.pallas_call(functools.partial(kernel, sizes), out_shape=(pltpu.VMEM((w...  59.5 us
    pallas_call x1, Pallas kernels, local(): pl.pallas_call(store, out_shape=(jax.ShapeDtypeStruct((width, rows), F32)...  1.65 us

profile of v1, /device:TPU:7, one launch (start us, length us, event | category | flops | bytes accessed | tf_op | source)
XLA Modules:
  0.0 63.7 jit_solution(17659070110528627977)
XLA Ops:
  1.3 59.5 %shard_map.158 = (f32[448,128]{1,0:T(8,128)S(1)}, bf16[128,128]{1,0:T(8,128)(2,1)S(1)}) custom-call(s32[2]{0:T(128)} %lengths_in.1, f32[64]{0:T(128)} %table_in.1, s32[1,1]{1,0:T(1,128)S(6)} %copy.17.chosen_in, f32[1,128]{1,0:T(1,128)} %attn_in.1, f32[1,128]{1,0:T(1,128)} %mlp_in.1, f32[1,128]{1,0:T(1,128)} %bias_in.1, s32[1,4096]{1,0:T(1,128)} %mode_in.1, ...), custom_call_target="tpu_custom_call" | custom-call | tf_op jit(solution)/shard_map/pallas_call | solution.py:493
  60.8 0.0 copy-start
  60.8 0.7 %copy-done = f32[448,128]{1,0:T(8,128)} copy-done((f32[448,128]{1,0:T(8,128)}, f32[448,128]{1,0:T(8,128)S(1)}, u32[]{:S(2)}) %copy-start) | copy-done | bytes 229400
  61.4 0.0 copy-start.1
  61.4 0.6 copy-done.1
  62.0 1.6 %shard_map.159 = (f32[448,128]{1,0:T(8,128)}, bf16[128,128]{1,0:T(8,128)(2,1)}) custom-call(f32[448,128]{1,0:T(8,128)} %copy-done, bf16[128,128]{1,0:T(8,128)(2,1)} %copy-done.1), custom_call_target="tpu_custom_call" | custom-call | tf_op jit(solution)/shard_map/pallas_call | solution.py:530
Async XLA Ops:
  60.8 0.7 %copy-start = (f32[448,128]{1,0:T(8,128)}, f32[448,128]{1,0:T(8,128)S(1)}, u32[]{:S(2)}) copy-start(f32[448,128]{1,0:T(8,128)S(1)} %get-tuple-element.6.x_ref) | copy-start | bytes 688132
  61.4 0.6 copy-start.1

commit v2 on v1

--- a/solution.py
+++ b/solution.py
@@ -24,11 +24,9 @@
     out_ref, feat_ref,
     lengths, table, chosen, scale_attn, scale_mlp, bias, mode_row, index_row,
     x_t, err_t, pat, wv, wo, we, wd,
-    xbuf, slots, relay_x, nbuf, masked, part_v, part_v2, vals, part_e, e_out, e_in, feats,
+    xbuf, slots, relay_x, nbuf, normed, masked, part_v, part_v2, vals, part_e, e_out, e_in, feats,
     acc_in, acc_out, att, err, wek, relay_in, relay_mid,
-    local_sem, xs_send, xs_recv, rx_send, ns_send, zx_send, zx_recv, zf_send, t_send, t_recv,
-    v_send, v_recv, vf_send, m_send, m_recv, f_send, f_recv, a_send, a_recv,
-    w_send, w_recv, b_send, b_recv,
+    local_sem, sent, xs_recv, zx_recv, t_recv, v_recv, m_recv, f_recv, a_recv, w_recv, b_recv,
 ):
     layers, feat_n, seq, prompts, head_dim, per_group, kv, width, block, rows, entries, shares = sizes
     half = seq // 2
@@ -79,9 +77,9 @@
         pl.when(me_l == 1)(lambda: greet({"groups": (me_g + g) % shares, "layer": prv}))
     greet({"tok": other})
 
-    def send(src, dst, ss, rs, where):
+    def send(src, dst, rs, where):
         return pltpu.make_async_remote_copy(
-            src_ref=src, dst_ref=dst, send_sem=ss, recv_sem=rs, device_id=where, device_id_type=mesh_id
+            src_ref=src, dst_ref=dst, send_sem=sent.at[0], recv_sem=rs, device_id=where, device_id_type=mesh_id
         )
 
     def peer(j):
@@ -103,8 +101,8 @@
         else:
             pl.when(cond)(copy.start)
 
-    def landed(ref, ss, rs):
-        send(ref, ref, ss, rs, {"tok": other}).wait_recv()
+    def landed(ref, rs):
+        send(ref, ref, rs, {"tok": other}).wait_recv()
 
     l_x.wait()
     x_rows = jnp.transpose(x_t[...])
@@ -126,10 +124,10 @@
         cond = both(both(to >= 0, to < feat_n), cond)
         to = jnp.clip(to, 0, feat_n - 1)
         slot = slots.at[p, me_f]
-        launch(send(slot, slot, xs_send.at[p, to], xs_recv.at[p, me_f], {"feat": to}), cond)
+        launch(send(slot, slot, xs_recv.at[p, me_f], {"feat": to}), cond)
 
     def x_landed(p, s):
-        landed(slots.at[p, s], xs_send.at[p, 0], xs_recv.at[p, s])
+        landed(slots.at[p, s], xs_recv.at[p, s])
 
     for p in streams:
         for step in (2, -2, 1, -1):
@@ -147,14 +145,14 @@
     first_up = [
         send(
             we.at[pl.ds(pl.multiple_of(peer(j) * width + my_share * share, 16), share)],
-            relay_in.at[peer(j), front], w_send.at[0, j], w_recv.at[0, peer(j)], {"layer": nxt},
+            relay_in.at[peer(j), front], w_recv.at[0, peer(j)], {"layer": nxt},
         )
         for j in range(1, feat_n)
     ]
     across = [
         send(
             relay_in.at[peer(j), front], relay_mid.at[me_f, front],
-            w_send.at[1, j], w_recv.at[1, me_f], {"feat": peer(j)},
+            w_recv.at[1, me_f], {"feat": peer(j)},
         )
         for j in range(1, feat_n)
     ]
@@ -163,7 +161,7 @@
             send(
                 relay_mid.at[peer(j), front],
                 wek.at[peer(j), pl.ds(pl.multiple_of(my_share * share, 16), share)],
-                b_send.at[g, j], b_recv.at[my_share, peer(j)],
+                b_recv.at[my_share, peer(j)],
                 {"layer": prv, "groups": (me_g + g) % shares} if g else {"layer": prv},
             )
             for g in range(shares)
@@ -171,13 +169,13 @@
         for j in range(1, feat_n)
     ]
     direct = [
-        send(we_rows(peer(j)), wek.at[me_f], w_send.at[3, j], w_recv.at[2, me_f], {"feat": peer(j)})
+        send(we_rows(peer(j)), wek.at[me_f], w_recv.at[2, me_f], {"feat": peer(j)})
         for j in range(1, feat_n)
     ]
 
     def w_arrived(ref, stage, s):
         part_ref = ref.at[s, front] if stage < 2 else ref.at[s]
-        send(part_ref, part_ref, w_send.at[stage, 0], w_recv.at[stage, s], {"tok": other}).wait_recv()
+        landed(part_ref, w_recv.at[stage, s])
 
     @pl.when(is_first)
     def _():
@@ -224,7 +222,7 @@
             masked[h // per_group, p, pl.ds(h % per_group * seq, seq), :] = jnp.where(
                 keep, pat[h, p].astype(F32), 0.0
             ).astype(BF16)
-        e_in[p, me_f, me_t] = jnp.zeros((half, block), BF16)
+        e_in[p, 2 * me_f + me_t] = jnp.zeros((half, block), BF16)
     own_rows.wait()
 
     for p in streams:
@@ -237,41 +235,66 @@
             for step in (feat_n - k, k - feat_n):
                 share_x(p, step, has_prev if abs(step) == 1 else both(has_prev, jnp.logical_not(at_end)))
 
+    def arrival(k):
+        return jnp.where(at_end, far(feat_n - 1 - k), far(k - 1)) if k else me_f
+
     for p in streams:
         total = jnp.zeros((seq, kv), F32)
-        for s in order:
-            pl.when(me_f != s)(lambda: x_landed(p, s))
-            for side, step in enumerate((1, -1)):
-                to = me_f + step
-                inside = both(to >= 0, to < feat_n)
-                if_far = (to - s) * step > 2
-                launch(
-                    send(
-                        slots.at[p, s], slots.at[p, s], rx_send.at[p, s, side], xs_recv.at[p, s],
-                        {"feat": jnp.clip(to, 0, feat_n - 1)},
-                    ),
-                    both(is_first, both(inside, if_far)),
-                )
-            total += jnp.dot(slots[p, s], wv[pl.ds(s * width, width), :], preferred_element_type=F32)
+        for k in range(feat_n):
+            s = arrival(k)
+            if k:
+                x_landed(p, s)
+                for step in (1, -1):
+                    to = me_f + step
+                    inside = both(to >= 0, to < feat_n)
+                    relays = both(is_first, both(inside, (to - s) * step > 2))
+                    to = jnp.clip(to, 0, feat_n - 1)
+                    launch(send(slots.at[p, s], slots.at[p, s], xs_recv.at[p, s], {"feat": to}), relays)
+            from_rows = pl.ds(pl.multiple_of(s * width, 16), width)
+            total += jnp.dot(slots[p, s], wv[from_rows, :], preferred_element_type=F32)
         total *= attn_col[p * seq : (p + 1) * seq]
         part_v[p] = total.reshape(2, half, kv)
-        launch(send(part_v.at[p, other], part_v2.at[p], t_send.at[p], t_recv.at[p], {"tok": other}))
-        landed(part_v2.at[p], t_send.at[p], t_recv.at[p])
+        launch(send(part_v.at[p, other], part_v2.at[p], t_recv.at[p], {"tok": other}))
+        landed(part_v2.at[p], t_recv.at[p])
         vals[p, me_f, me_t] = (part_v[p, me_t] + part_v2[p]).astype(BF16)
         mine = vals.at[p, me_f, me_t]
         for k in range(feat_n - 1):
-            launch(send(mine, mine, v_send.at[p, k], v_recv.at[p, me_f, me_t], {"feat": far(k)}))
-        launch(send(mine, mine, vf_send.at[p, me_f], v_recv.at[p, me_f, me_t], {"tok": other}))
+            launch(send(mine, mine, v_recv.at[p, me_f, me_t], {"feat": far(k)}))
+        launch(send(mine, mine, v_recv.at[p, me_f, me_t], {"tok": other}))
 
     def take(p, s):
         got = vals.at[p, s, me_t]
-
-        @pl.when(me_f != s)
+        pl.when(me_f != s)(lambda: landed(got, v_recv.at[p, s, me_t]))
+        launch(send(got, got, v_recv.at[p, s, me_t], {"tok": other}), me_f != s)
+
+    def encode(p, cond):
+        @pl.when(cond)
         def _():
-            landed(got, vf_send.at[p, s], v_recv.at[p, s, me_t])
-            send(got, got, vf_send.at[p, s], v_recv.at[p, s, me_t], {"tok": other}).start()
-
-        pending.append((send(got, got, vf_send.at[p, s], v_recv.at[p, s, me_t], {"tok": other}), me_f != s))
+            normed_mlp = normed[p]
+            for k in range(feat_n):
+                to = far(k) if k < feat_n - 1 else me_f
+                result = jnp.dot(normed_mlp, wek[to], preferred_element_type=F32).reshape(2, half, block)
+                for t in range(2):
+                    e_out[p, 2 * k + t] = result[t].astype(BF16)
+                if k < feat_n - 1:
+                    for t in range(2):
+                        e_send(p, k, t).start()
+                else:
+                    part_e[p] = result
+                    e_swap(p).start()
+
+    def e_send(p, k, t):
+        return send(e_out.at[p, 2 * k + t], e_in.at[p, 2 * me_f + me_t], m_recv.at[p], {"feat": far(k), "tok": t})
+
+    def e_swap(p):
+        mine = 2 * (feat_n - 1) + other
+        return send(e_out.at[p, mine], e_in.at[p, 2 * me_f + me_t], m_recv.at[p], {"tok": other})
+
+    for p in streams:
+        for k in range(feat_n - 1):
+            for t in range(2):
+                pending.append((e_send(p, k, t), None))
+        pending.append((e_swap(p), None))
 
     for p in streams:
         total = jnp.zeros((seq, width), F32)
@@ -281,7 +304,7 @@
             if n == 0:
                 continue
             s = order[n - 1]
-            landed(vals.at[p, s, other], vf_send.at[p, s], v_recv.at[p, s, other])
+            landed(vals.at[p, s, other], v_recv.at[p, s, other])
             group = s * kv // head_dim
             d0 = s * kv % head_dim
             heads = jnp.dot(masked[group, p], vals[p, s].reshape(seq, kv), preferred_element_type=F32).astype(BF16)
@@ -289,69 +312,45 @@
                 total += lax.dot_general(
                     heads[u * seq : (u + 1) * seq], wo[group, u, :, pl.ds(d0, kv)], NT, preferred_element_type=F32
                 )
-
+        middle = xbuf[p] + total
+        normed[p] = (middle * mlp_col[p * seq : (p + 1) * seq]).astype(BF16)
+        att[part(p), :] = middle + err[part(p), :]
         if p == 0:
             for s in range(feat_n):
-                @pl.when(both(has_prev, me_f != s))
-                def _():
-                    w_arrived(wek, 2, s)
-
-                @pl.when(both(is_first, me_f != s))
-                def _():
-                    for g in range(shares):
-                        here = wek.at[s, pl.ds(g * share, share)]
-                        send(here, here, b_send.at[0, 0], b_recv.at[g, s], {"tok": other}).wait_recv()
-
-        middle = xbuf[p] + total
-        normed_mlp = (middle * mlp_col[p * seq : (p + 1) * seq]).astype(BF16)
-        for k in range(feat_n):
-            to = far(k) if k < feat_n - 1 else me_f
-            result = jnp.dot(normed_mlp, wek[to], preferred_element_type=F32).reshape(2, half, block)
-            e_out[p, k] = result.astype(BF16)
-            if k < feat_n - 1:
-                for t in range(2):
-                    launch(
-                        send(
-                            e_out.at[p, k, t], e_in.at[p, me_f, me_t], m_send.at[p, k, t],
-                            m_recv.at[p, me_f, me_t], {"feat": to, "tok": t},
-                        )
-                    )
-            else:
-                part_e[p] = result
-                launch(
-                    send(
-                        e_out.at[p, k, other], e_in.at[p, me_f, me_t], m_send.at[p, k, 0],
-                        m_recv.at[p, me_f, me_t], {"tok": other},
-                    )
-                )
-        att[part(p), :] = middle + err[part(p), :]
-
-    def await_others(ref, ss, rs, p, s):
-        for t in range(2):
-            pl.when(jnp.logical_or(me_f != s, me_t != t))(
-                lambda: landed(ref.at[p, s, t], ss.at[p, 0, 0], rs.at[p, s, t])
+                pl.when(both(has_prev, me_f != s))(lambda: w_arrived(wek, 2, s))
+        encode(p, has_prev)
+
+    for s in range(feat_n):
+        for g in range(shares):
+            pl.when(both(is_first, me_f != s))(
+                lambda: landed(wek.at[s, pl.ds(g * share, share)], b_recv.at[g, s])
             )
-
-    for p in streams:
-        for s in order:
-            await_others(e_in, m_send, m_recv, p, s)
+    for p in streams:
+        encode(p, is_first)
+
+    def await_others(ref, rs):
+        landed(ref.at[pl.ds(0, 2 * feat_n - 1)], rs)
+
+    for p in streams:
+        await_others(e_in.at[p], m_recv.at[p])
         preact = part_e[p, me_t] + shift
-        for s in range(feat_n):
-            for t in range(2):
-                preact += e_in[p, s, t].astype(F32)
+        for s in range(2 * feat_n):
+            preact += e_in[p, s].astype(F32)
         active = jnp.maximum(preact, 0.0)
         clamped = jnp.where(modes == 1, levels, jnp.where(modes == 2, active * levels, active))
-        feats[p, me_f, me_t] = jnp.where(lives[p], clamped, 0.0).astype(BF16)
-        mine = feats.at[p, me_f, me_t]
+        here = 2 * me_f + me_t
+        feats[p, here] = jnp.where(lives[p], clamped, 0.0).astype(BF16)
+        mine = feats.at[p, here]
         for k in range(feat_n - 1):
             for t in range(2):
-                launch(
-                    send(mine, mine, f_send.at[p, k, t], f_recv.at[p, me_f, me_t], {"feat": far(k), "tok": t})
-                )
-        launch(send(mine, mine, f_send.at[p, feat_n - 1, 0], f_recv.at[p, me_f, me_t], {"tok": other}))
+                launch(send(mine, mine, f_recv.at[p], {"feat": far(k), "tok": t}))
+        launch(send(mine, mine, f_recv.at[p], {"tok": other}))
+
+    def features(p, s):
+        return feats[p, 2 * s : 2 * s + 2].reshape(seq, block)
 
     def acc_copy(p, t):
-        return send(acc_out.at[p, t], acc_in.at[p, t], a_send.at[p, t], a_recv.at[p, t], {"layer": nxt})
+        return send(acc_out.at[p, t], acc_in.at[p, t], a_recv.at[p, t], {"layer": nxt})
 
     for p in streams:
         @pl.when(has_prev)
@@ -363,14 +362,13 @@
             att[part(p), :] += acc_in[p, me_l]
 
         total = att[part(p), :]
-        for s in order:
-            await_others(feats, f_send, f_recv, p, s)
+        await_others(feats.at[p], f_recv.at[p])
+        for s in range(feat_n):
             total += lax.dot_general(
-                feats[p, s].reshape(seq, block), wd[me_l, :, pl.ds(s * block, block)], NT,
-                preferred_element_type=F32,
+                features(p, s), wd[me_l, :, pl.ds(s * block, block)], NT, preferred_element_type=F32
             )
         att[part(p), :] = total
-        feat_ref[part(p), :] = feats[p, me_f].reshape(seq, block)
+        feat_ref[part(p), :] = feats[p, pl.ds(2 * me_f, 2)].reshape(seq, block)
 
         @pl.when(has_next)
         def _():
@@ -380,21 +378,18 @@
             to = jnp.where(me_f == 0, feat_n - 1 - k, k)
             launch(
                 send(
-                    nbuf.at[p], relay_x.at[p, jnp.minimum(me_f, 1)], zx_send.at[p, k],
-                    zx_recv.at[p, jnp.minimum(me_f, 1)], {"feat": to},
+                    nbuf.at[p], relay_x.at[p, jnp.minimum(me_f, 1)], zx_recv.at[p, jnp.minimum(me_f, 1)],
+                    {"feat": to},
                 ),
                 both(has_next, at_end),
             )
-        launch(send(nbuf.at[p], slots.at[p, me_f], ns_send.at[p], xs_recv.at[p, me_f], {"layer": nxt}), has_next)
+        launch(send(nbuf.at[p], slots.at[p, me_f], xs_recv.at[p, me_f], {"layer": nxt}), has_next)
 
     for p in streams:
         for e, src in enumerate(ends):
             relays = both(has_next, jnp.abs(me_f - src) > 1)
-            pl.when(relays)(lambda: landed(relay_x.at[p, e], zx_send.at[p, 0], zx_recv.at[p, e]))
-            launch(
-                send(relay_x.at[p, e], slots.at[p, src], zf_send.at[p, e], xs_recv.at[p, src], {"layer": nxt}),
-                relays,
-            )
+            pl.when(relays)(lambda: landed(relay_x.at[p, e], zx_recv.at[p, e]))
+            launch(send(relay_x.at[p, e], slots.at[p, src], xs_recv.at[p, src], {"layer": nxt}), relays)
 
     @pl.when(has_next)
     def _():
@@ -406,7 +401,7 @@
                     total = jnp.where(me_l + 1 == t, rest, 0.0)
                     for s in range(feat_n):
                         total += lax.dot_general(
-                            feats[p, s].reshape(seq, block), wd[t, :, pl.ds(s * block, block)], NT,
+                            features(p, s), wd[t, :, pl.ds(s * block, block)], NT,
                             preferred_element_type=F32,
                         )
                     acc_out[p, t] = total
@@ -502,31 +497,29 @@
             pltpu.VMEM((prompts, feat_n, seq, width), BF16),
             pltpu.VMEM((prompts, 2, seq, width), BF16),
             pltpu.VMEM((prompts, seq, width), BF16),
+            pltpu.VMEM((prompts, seq, width), BF16),
             pltpu.VMEM((kv_heads, prompts, per_group * seq, seq), BF16),
             pltpu.VMEM((prompts, 2, half, kv), F32),
             pltpu.VMEM((prompts, half, kv), F32),
             pltpu.VMEM((prompts, feat_n, 2, half, kv), BF16),
             pltpu.VMEM((prompts, 2, half, block), F32),
-            pltpu.VMEM((prompts, feat_n, 2, half, block), BF16),
-            pltpu.VMEM((prompts, feat_n, 2, half, block), BF16),
-            pltpu.VMEM((prompts, feat_n, 2, half, block), BF16),
+            pltpu.VMEM((prompts, 2 * feat_n, half, block), BF16),
+            pltpu.VMEM((prompts, 2 * feat_n, half, block), BF16),
+            pltpu.VMEM((prompts, 2 * feat_n, half, block), BF16),
             pltpu.VMEM((prompts, layers, seq, width), F32),
             pltpu.VMEM((prompts, layers, seq, width), F32),
             pltpu.VMEM((rows, width), F32),
             pltpu.VMEM((rows, width), F32),
         ]
         + [pltpu.VMEM((feat_n, width, block), BF16)] * 3
-        + [dma((16,))]
-        + [dma((prompts, feat_n))] * 2
-        + [dma((prompts, feat_n, 2)), dma((prompts,)), dma((prompts, feat_n)), dma((prompts, 2)), dma((prompts, 2))]
-        + [dma((prompts,))] * 2
-        + [dma((prompts, feat_n)), dma((prompts, feat_n, 2)), dma((prompts, feat_n))]
-        + [dma((prompts, feat_n, 2))] * 4
-        + [dma((prompts, layers))] * 2
-        + [dma((4, feat_n)), dma((3, feat_n))]
-        + [dma((shares, feat_n))] * 2,
+        + [
+            dma((16,)), dma((1,)), dma((prompts, feat_n)), dma((prompts, 2)), dma((prompts,)),
+            dma((prompts, feat_n, 2)), dma((prompts,)), dma((prompts,)), dma((prompts, layers)),
+            dma((3, feat_n)), dma((shares, feat_n)),
+        ],
         compiler_params=pltpu.CompilerParams(collective_id=0, has_side_effects=True),
     )(*small, *big)
+    out_t, out_f = (pltpu.with_memory_space_constraint(a, pltpu.VMEM) for a in (out_t, out_f))
     out_t, out_f = pl.pallas_call(
         store,
         out_shape=(

time: 64 us -> 61.5 us (0.961)
  Pallas kernels: 61.1 us -> 59.4 us
  local copies, waits for them, and re-layouts: 1.27 us -> 0 us
    unnamed x4 -> x0, local copies, waits for them, and re-layouts: 1.27 us -> none
    pallas_call x1, Pallas kernels: 1.65 us -> 0.71 us  [local(): pl.pallas_call(store, out_shape=(jax.ShapeDtypeStruct((width, rows), F32)...]
    pallas_call x1, Pallas kernels: 59.5 us -> 58.6 us  [local(): pl.pallas_call(functools.partial(kernel, sizes), out_shape=(pltpu.VMEM((w...]
where the time goes in v2:
time: 61.5 us; the launch traced here: 60.6 us
  Pallas kernels  59.4 us (97%)
  between operations  1.29 us (2%)
    pallas_call x1, Pallas kernels, local(): pl.pallas_call(functools.partial(kernel, sizes), out_shape=(pltpu.VMEM((w...  58.6 us

profile of v2, /device:TPU:7, one launch (start us, length us, event | category | flops | bytes accessed | tf_op | source)
XLA Modules:
  0.0 60.6 jit_solution(846150500000709747)
XLA Ops:
  1.3 58.6 %shard_map.158 = (f32[448,128]{1,0:T(8,128)S(1)}, bf16[128,128]{1,0:T(8,128)(2,1)S(1)}) custom-call(s32[2]{0:T(128)} %lengths_in.1, f32[64]{0:T(128)} %table_in.1, s32[1,1]{1,0:T(1,128)S(6)} %copy.17.chosen_in, f32[1,128]{1,0:T(1,128)} %attn_in.1, f32[1,128]{1,0:T(1,128)} %mlp_in.1, f32[1,128]{1,0:T(1,128)} %bias_in.1, s32[1,4096]{1,0:T(1,128)} %mode_in.1, ...), custom_call_target="tpu_custom_call" | custom-call | tf_op jit(solution)/shard_map/pallas_call | solution.py:488
  59.9 0.7 %shard_map.159 = (f32[448,128]{1,0:T(8,128)}, bf16[128,128]{1,0:T(8,128)(2,1)}) custom-call(f32[448,128]{1,0:T(8,128)S(1)} %get-tuple-element.6.x_ref, bf16[128,128]{1,0:T(8,128)(2,1)S(1)} %get-tuple-element.7.f_ref), custom_call_target="tpu_custom_call" | custom-call | tf_op jit(solution)/shard_map/pallas_call | solution.py:523

commit v3 on v2

--- a/solution.py
+++ b/solution.py
@@ -24,9 +24,9 @@
     out_ref, feat_ref,
     lengths, table, chosen, scale_attn, scale_mlp, bias, mode_row, index_row,
     x_t, err_t, pat, wv, wo, we, wd,
-    xbuf, slots, relay_x, nbuf, normed, masked, part_v, part_v2, vals, part_e, e_out, e_in, feats,
+    xbuf, slots, nbuf, normed, masked, part_v, part_v2, vals, part_e, e_out, e_in, feats,
     acc_in, acc_out, att, err, wek, relay_in, relay_mid,
-    local_sem, sent, xs_recv, zx_recv, t_recv, v_recv, m_recv, f_recv, a_recv, w_recv, b_recv,
+    local_sem, sent, up_sent, own_recv, xs_recv, t_recv, v_recv, m_recv, f_recv, a_recv, w_recv, b_recv,
 ):
     layers, feat_n, seq, prompts, head_dim, per_group, kv, width, block, rows, entries, shares = sizes
     half = seq // 2
@@ -41,7 +41,6 @@
     nxt = jnp.minimum(me_l + 1, layers - 1)
     prv = jnp.maximum(me_l - 1, 0)
     streams = range(prompts)
-    ends = (0, feat_n - 1)
     at_end = jnp.logical_or(me_f == 0, me_f == feat_n - 1)
     order = sorted(range(feat_n), key=lambda s: abs(2 * s - feat_n + 1))
     low_side = 2 * me_f < feat_n
@@ -71,7 +70,8 @@
         for t in range(2):
             greet({"feat": (me_f + j) % feat_n, "tok": t})
     pl.when(has_next)(lambda: greet({"layer": nxt}))
-    pl.when(has_prev)(lambda: greet({"layer": prv}))
+    for s in range(feat_n):
+        pl.when(both(has_prev, jnp.abs(me_f - s) != 1))(lambda: greet({"layer": prv, "feat": s}))
     for g in range(1, shares):
         pl.when(is_first)(lambda: greet({"groups": (me_g + g) % shares, "layer": nxt}))
         pl.when(me_l == 1)(lambda: greet({"groups": (me_g + g) % shares, "layer": prv}))
@@ -115,9 +115,8 @@
             xbuf[p] = x_rows[p * seq : (p + 1) * seq]
 
     extra = (shares - 1) * (1 - jnp.minimum(me_l // 2, 1))
-    pl.semaphore_wait(
-        barrier, 2 * feat_n - 1 + jnp.minimum(me_l, 1) + jnp.minimum(layers - 1 - me_l, 1) + extra
-    )
+    above = jnp.minimum(layers - 1 - me_l, 1) * (feat_n - 2 + jnp.where(at_end, 1, 0))
+    pl.semaphore_wait(barrier, 2 * feat_n - 1 + jnp.minimum(me_l, 1) + above + extra)
 
     def share_x(p, step, cond):
         to = me_f + step
@@ -129,9 +128,11 @@
     def x_landed(p, s):
         landed(slots.at[p, s], xs_recv.at[p, s])
 
-    for p in streams:
+    def share_first(p):
         for step in (2, -2, 1, -1):
             share_x(p, step, is_first)
+
+    share_first(0)
 
     def we_rows(s):
         return we.at[pl.ds(pl.multiple_of(s * width, 16), width)]
@@ -177,25 +178,25 @@
         part_ref = ref.at[s, front] if stage < 2 else ref.at[s]
         landed(part_ref, w_recv.at[stage, s])
 
-    @pl.when(is_first)
-    def _():
-        for copy in first_up:
-            copy.start()
-
-    @pl.when(me_l == 1)
-    def _():
-        for j in range(1, feat_n):
-            w_arrived(relay_in, 0, peer(j))
-            across[j - 1].start()
-        for j in range(1, feat_n):
-            w_arrived(relay_mid, 1, peer(j))
-            for copy in back[j - 1]:
-                copy.start()
-
-    @pl.when(has_prev)
-    def _():
-        for copy in direct:
-            copy.start()
+    def distant(j):
+        return jnp.abs(peer(j) - me_f) > 1
+
+    def next_to(j):
+        return jnp.abs(peer(j) - me_f) == 1
+
+    for j in range(1, feat_n):
+        launch(first_up[j - 1], both(is_first, distant(j)))
+    for j in range(1, feat_n):
+        relays = both(me_l == 1, distant(j))
+        pl.when(relays)(lambda: w_arrived(relay_in, 0, peer(j)))
+        launch(across[j - 1], relays)
+    for j in range(1, feat_n):
+        relays = both(me_l == 1, distant(j))
+        pl.when(relays)(lambda: w_arrived(relay_mid, 1, peer(j)))
+        for copy in back[j - 1]:
+            launch(copy, relays)
+    for j in range(1, feat_n):
+        launch(direct[j - 1], has_prev)
 
     for load in loads[2:]:
         load.wait()
@@ -226,20 +227,39 @@
     own_rows.wait()
 
     for p in streams:
+        for h in range(2):
+            slot = slots.at[p, me_f, pl.ds(h * half, half)]
+            pl.when(has_prev)(lambda: landed(slot, own_recv.at[p, h]))
+            for step in (1, -1):
+                to = me_f + step
+                inside = both(has_prev, both(to >= 0, to < feat_n))
+                launch(send(slot, slot, xs_recv.at[p, me_f], {"feat": jnp.clip(to, 0, feat_n - 1)}), inside)
+
         @pl.when(has_prev)
         def _():
-            x_landed(p, me_f)
             xbuf[p] = slots[p, me_f].astype(F32)
-
-        for k in range(1, feat_n):
-            for step in (feat_n - k, k - feat_n):
-                share_x(p, step, has_prev if abs(step) == 1 else both(has_prev, jnp.logical_not(at_end)))
 
     def arrival(k):
         return jnp.where(at_end, far(feat_n - 1 - k), far(k - 1)) if k else me_f
 
+    def v_sends(p):
+        mine = vals.at[p, me_f]
+        return [send(mine, mine, v_recv.at[p, me_f], {"feat": far(k)}) for k in range(feat_n - 1)]
+
+    def v_finish(p, cond):
+        @pl.when(cond)
+        def _():
+            landed(part_v2.at[p], t_recv.at[p])
+            vals[p, me_f] = (part_v[p] + part_v2[p]).astype(BF16)
+            for copy in v_sends(p):
+                copy.start()
+
+    relaying = both(is_first, jnp.logical_not(at_end))
     for p in streams:
+        pending.extend((copy, None) for copy in v_sends(p))
         total = jnp.zeros((seq, kv), F32)
+        if p:
+            v_finish(p - 1, jnp.logical_not(relaying))
         for k in range(feat_n):
             s = arrival(k)
             if k:
@@ -250,38 +270,32 @@
                     relays = both(is_first, both(inside, (to - s) * step > 2))
                     to = jnp.clip(to, 0, feat_n - 1)
                     launch(send(slots.at[p, s], slots.at[p, s], xs_recv.at[p, s], {"feat": to}), relays)
+            if k == 1:
+                if p + 1 < prompts:
+                    share_first(p + 1)
+                if p:
+                    v_finish(p - 1, relaying)
+                if p + 1 == prompts:
+                    for j in range(1, feat_n):
+                        launch(direct[j - 1], both(is_first, next_to(j)))
             from_rows = pl.ds(pl.multiple_of(s * width, 16), width)
             total += jnp.dot(slots[p, s], wv[from_rows, :], preferred_element_type=F32)
         total *= attn_col[p * seq : (p + 1) * seq]
-        part_v[p] = total.reshape(2, half, kv)
-        launch(send(part_v.at[p, other], part_v2.at[p], t_recv.at[p], {"tok": other}))
-        landed(part_v2.at[p], t_recv.at[p])
-        vals[p, me_f, me_t] = (part_v[p, me_t] + part_v2[p]).astype(BF16)
-        mine = vals.at[p, me_f, me_t]
-        for k in range(feat_n - 1):
-            launch(send(mine, mine, v_recv.at[p, me_f, me_t], {"feat": far(k)}))
-        launch(send(mine, mine, v_recv.at[p, me_f, me_t], {"tok": other}))
-
-    def take(p, s):
-        got = vals.at[p, s, me_t]
-        pl.when(me_f != s)(lambda: landed(got, v_recv.at[p, s, me_t]))
-        launch(send(got, got, v_recv.at[p, s, me_t], {"tok": other}), me_f != s)
-
-    def encode(p, cond):
-        @pl.when(cond)
-        def _():
-            normed_mlp = normed[p]
-            for k in range(feat_n):
-                to = far(k) if k < feat_n - 1 else me_f
-                result = jnp.dot(normed_mlp, wek[to], preferred_element_type=F32).reshape(2, half, block)
-                for t in range(2):
-                    e_out[p, 2 * k + t] = result[t].astype(BF16)
+        part_v[p] = total
+        launch(send(part_v.at[p], part_v2.at[p], t_recv.at[p], {"tok": other}))
+    v_finish(prompts - 1, me_f >= 0)
+
+    def encode(p):
+        for k in range(feat_n):
+            to = far(k) if k < feat_n - 1 else me_f
+            result = jnp.dot(normed[part(p), :], wek[to], preferred_element_type=F32).reshape(2, half, block)
+            for t in range(2):
+                e_out[p, 2 * k + t] = result[t].astype(BF16)
                 if k < feat_n - 1:
-                    for t in range(2):
-                        e_send(p, k, t).start()
-                else:
-                    part_e[p] = result
-                    e_swap(p).start()
+                    launch(e_send(p, k, t))
+            if k == feat_n - 1:
+                part_e[p] = result
+                launch(e_swap(p))
 
     def e_send(p, k, t):
         return send(e_out.at[p, 2 * k + t], e_in.at[p, 2 * me_f + me_t], m_recv.at[p], {"feat": far(k), "tok": t})
@@ -291,42 +305,29 @@
         return send(e_out.at[p, mine], e_in.at[p, 2 * me_f + me_t], m_recv.at[p], {"tok": other})
 
     for p in streams:
-        for k in range(feat_n - 1):
-            for t in range(2):
-                pending.append((e_send(p, k, t), None))
-        pending.append((e_swap(p), None))
-
-    for p in streams:
         total = jnp.zeros((seq, width), F32)
-        for n in range(feat_n + 1):
-            if n < feat_n:
-                take(p, order[n])
-            if n == 0:
-                continue
-            s = order[n - 1]
-            landed(vals.at[p, s, other], v_recv.at[p, s, other])
+        for s in order:
+            pl.when(me_f != s)(lambda: landed(vals.at[p, s], v_recv.at[p, s]))
             group = s * kv // head_dim
             d0 = s * kv % head_dim
-            heads = jnp.dot(masked[group, p], vals[p, s].reshape(seq, kv), preferred_element_type=F32).astype(BF16)
+            heads = jnp.dot(masked[group, p], vals[p, s], preferred_element_type=F32).astype(BF16)
             for u in range(per_group):
                 total += lax.dot_general(
                     heads[u * seq : (u + 1) * seq], wo[group, u, :, pl.ds(d0, kv)], NT, preferred_element_type=F32
                 )
         middle = xbuf[p] + total
-        normed[p] = (middle * mlp_col[p * seq : (p + 1) * seq]).astype(BF16)
+        normed[part(p), :] = (middle * mlp_col[p * seq : (p + 1) * seq]).astype(BF16)
         att[part(p), :] = middle + err[part(p), :]
         if p == 0:
             for s in range(feat_n):
-                pl.when(both(has_prev, me_f != s))(lambda: w_arrived(wek, 2, s))
-        encode(p, has_prev)
-
-    for s in range(feat_n):
-        for g in range(shares):
-            pl.when(both(is_first, me_f != s))(
-                lambda: landed(wek.at[s, pl.ds(g * share, share)], b_recv.at[g, s])
-            )
-    for p in streams:
-        encode(p, is_first)
+                apart = jnp.abs(me_f - s)
+                straight = jnp.logical_or(both(has_prev, apart > 0), apart == 1)
+                pl.when(straight)(lambda: w_arrived(wek, 2, s))
+                for g in range(shares):
+                    pl.when(both(is_first, apart > 1))(
+                        lambda: landed(wek.at[s, pl.ds(g * share, share)], b_recv.at[g, s])
+                    )
+        encode(p)
 
     def await_others(ref, rs):
         landed(ref.at[pl.ds(0, 2 * feat_n - 1)], rs)
@@ -349,6 +350,13 @@
     def features(p, s):
         return feats[p, 2 * s : 2 * s + 2].reshape(seq, block)
 
+    def x_up(p, h):
+        part_h = pl.ds(h * half, half)
+        return pltpu.make_async_remote_copy(
+            src_ref=nbuf.at[p, part_h], dst_ref=slots.at[p, me_f, part_h], send_sem=up_sent.at[p],
+            recv_sem=own_recv.at[p, h], device_id={"layer": nxt}, device_id_type=mesh_id,
+        )
+
     def acc_copy(p, t):
         return send(acc_out.at[p, t], acc_in.at[p, t], a_recv.at[p, t], {"layer": nxt})
 
@@ -374,22 +382,14 @@
         def _():
             nbuf[p] = att[part(p), :].astype(BF16)
 
-        for k in range(feat_n - 2):
-            to = jnp.where(me_f == 0, feat_n - 1 - k, k)
+        for h in range(2):
+            pl.when(has_next)(x_up(p, h).start)
+        for k in range(feat_n - 1):
+            to = far(k)
             launch(
-                send(
-                    nbuf.at[p], relay_x.at[p, jnp.minimum(me_f, 1)], zx_recv.at[p, jnp.minimum(me_f, 1)],
-                    {"feat": to},
-                ),
-                both(has_next, at_end),
+                send(nbuf.at[p], slots.at[p, me_f], xs_recv.at[p, me_f], {"layer": nxt, "feat": to}),
+                both(has_next, jnp.abs(to - me_f) > 1),
             )
-        launch(send(nbuf.at[p], slots.at[p, me_f], xs_recv.at[p, me_f], {"layer": nxt}), has_next)
-
-    for p in streams:
-        for e, src in enumerate(ends):
-            relays = both(has_next, jnp.abs(me_f - src) > 1)
-            pl.when(relays)(lambda: landed(relay_x.at[p, e], zx_recv.at[p, e]))
-            launch(send(relay_x.at[p, e], slots.at[p, src], xs_recv.at[p, src], {"layer": nxt}), relays)
 
     @pl.when(has_next)
     def _():
@@ -410,24 +410,14 @@
                     def _():
                         acc_out[p, t] += acc_in[p, t]
 
-                    acc_copy(p, t).start()
+        for p in streams:
+            for h in range(2):
+                x_up(p, h).wait_send()
+        for p in streams:
+            for t in range(1, layers):
+                pl.when(t > me_l)(lambda: acc_copy(p, t).start())
 
     out_ref[...] = jnp.transpose(att[...])
-
-    @pl.when(is_first)
-    def _():
-        for copy in first_up:
-            copy.wait_send()
-
-    @pl.when(me_l == 1)
-    def _():
-        for copy in sum(back, across):
-            copy.wait_send()
-
-    @pl.when(has_prev)
-    def _():
-        for copy in direct:
-            copy.wait_send()
 
     for copy, cond in pending:
         if cond is None:
@@ -495,13 +485,12 @@
         + [
             pltpu.VMEM((prompts, seq, width), F32),
             pltpu.VMEM((prompts, feat_n, seq, width), BF16),
-            pltpu.VMEM((prompts, 2, seq, width), BF16),
             pltpu.VMEM((prompts, seq, width), BF16),
-            pltpu.VMEM((prompts, seq, width), BF16),
+            pltpu.VMEM((rows, width), BF16),
             pltpu.VMEM((kv_heads, prompts, per_group * seq, seq), BF16),
-            pltpu.VMEM((prompts, 2, half, kv), F32),
-            pltpu.VMEM((prompts, half, kv), F32),
-            pltpu.VMEM((prompts, feat_n, 2, half, kv), BF16),
+            pltpu.VMEM((prompts, seq, kv), F32),
+            pltpu.VMEM((prompts, seq, kv), F32),
+            pltpu.VMEM((prompts, feat_n, seq, kv), BF16),
             pltpu.VMEM((prompts, 2, half, block), F32),
             pltpu.VMEM((prompts, 2 * feat_n, half, block), BF16),
             pltpu.VMEM((prompts, 2 * feat_n, half, block), BF16),
@@ -513,8 +502,8 @@
         ]
         + [pltpu.VMEM((feat_n, width, block), BF16)] * 3
         + [
-            dma((16,)), dma((1,)), dma((prompts, feat_n)), dma((prompts, 2)), dma((prompts,)),
-            dma((prompts, feat_n, 2)), dma((prompts,)), dma((prompts,)), dma((prompts, layers)),
+            dma((16,)), dma((1,)), dma((prompts,)), dma((prompts, 2)), dma((prompts, feat_n)), dma((prompts,)),
+            dma((prompts, feat_n)), dma((prompts,)), dma((prompts,)), dma((prompts, layers)),
             dma((3, feat_n)), dma((shares, feat_n)),
         ],
         compiler_params=pltpu.CompilerParams(collective_id=0, has_side_effects=True),

time: 61.5 us -> 58.2 us (0.946)
  Pallas kernels: 59.4 us -> 56.7 us
    pallas_call x1, Pallas kernels: 58.6 us -> 55.9 us  [local(): pl.pallas_call(functools.partial(kernel, sizes), out_shape=(pltpu.VMEM((w...]
where the time goes in v3:
time: 58.2 us; the launch traced here: 57.9 us
  Pallas kernels  56.7 us (97%)
  between operations  1.29 us (2%)
    pallas_call x1, Pallas kernels, local(): pl.pallas_call(functools.partial(kernel, sizes), out_shape=(pltpu.VMEM((w...  55.9 us

profile of v3, /device:TPU:7, one launch (start us, length us, event | category | flops | bytes accessed | tf_op | source)
XLA Modules:
  0.0 57.9 jit_solution(17513996623257932351)
XLA Ops:
  1.3 55.9 %shard_map.158 = (f32[448,128]{1,0:T(8,128)S(1)}, bf16[128,128]{1,0:T(8,128)(2,1)S(1)}) custom-call(s32[2]{0:T(128)} %lengths_in.1, f32[64]{0:T(128)} %table_in.1, s32[1,1]{1,0:T(1,128)S(6)} %copy.17.chosen_in, f32[1,128]{1,0:T(1,128)} %attn_in.1, f32[1,128]{1,0:T(1,128)} %mlp_in.1, f32[1,128]{1,0:T(1,128)} %bias_in.1, s32[1,4096]{1,0:T(1,128)} %mode_in.1, ...), custom_call_target="tpu_custom_call" | custom-call | tf_op jit(solution)/shard_map/pallas_call | solution.py:478
  57.2 0.7 %shard_map.159 = (f32[448,128]{1,0:T(8,128)}, bf16[128,128]{1,0:T(8,128)(2,1)}) custom-call(f32[448,128]{1,0:T(8,128)S(1)} %get-tuple-element.6.x_ref, bf16[128,128]{1,0:T(8,128)(2,1)S(1)} %get-tuple-element.7.f_ref), custom_call_target="tpu_custom_call" | custom-call | tf_op jit(solution)/shard_map/pallas_call | solution.py:512

commit v4 on v3

--- a/solution.py
+++ b/solution.py
@@ -47,7 +47,7 @@
     both = jnp.logical_and
 
     loads = [
-        pltpu.make_async_copy(src, dst, local_sem.at[i])
+        pltpu.make_async_copy(src, dst, local_sem.at[min(i, 2)])
         for i, (src, dst) in enumerate(
             (
                 (x_in, x_t), (we_in, we), (attn_in, scale_attn), (lengths_in, lengths), (table_in, table),
@@ -138,7 +138,7 @@
         return we.at[pl.ds(pl.multiple_of(s * width, 16), width)]
 
     l_we.wait()
-    own_rows = pltpu.make_async_copy(we_rows(me_f), wek.at[me_f], local_sem.at[len(loads)])
+    own_rows = pltpu.make_async_copy(we_rows(me_f), wek.at[me_f], local_sem.at[3])
     own_rows.start()
     share = width // shares
     my_share = me_g if shares > 1 else 0
@@ -347,8 +347,16 @@
                 launch(send(mine, mine, f_recv.at[p], {"feat": far(k), "tok": t}))
         launch(send(mine, mine, f_recv.at[p], {"tok": other}))
 
-    def features(p, s):
-        return feats[p, 2 * s : 2 * s + 2].reshape(seq, block)
+    pair = 2 if feat_n % 2 == 0 else 1
+
+    def decode(p, t, total):
+        for s in range(0, feat_n, pair):
+            lhs = [feats[p, 2 * i : 2 * i + 2].reshape(seq, block) for i in range(s, s + pair)]
+            total += lax.dot_general(
+                jnp.concatenate(lhs, axis=1), wd[t, :, pl.ds(s * block, pair * block)], NT,
+                preferred_element_type=F32,
+            )
+        return total
 
     def x_up(p, h):
         part_h = pl.ds(h * half, half)
@@ -358,7 +366,7 @@
         )
 
     def acc_copy(p, t):
-        return send(acc_out.at[p, t], acc_in.at[p, t], a_recv.at[p, t], {"layer": nxt})
+        return send(acc_out.at[p, t], acc_in.at[p, t], a_recv.at[p, t - 1], {"layer": nxt})
 
     for p in streams:
         @pl.when(has_prev)
@@ -371,11 +379,7 @@
 
         total = att[part(p), :]
         await_others(feats.at[p], f_recv.at[p])
-        for s in range(feat_n):
-            total += lax.dot_general(
-                features(p, s), wd[me_l, :, pl.ds(s * block, block)], NT, preferred_element_type=F32
-            )
-        att[part(p), :] = total
+        att[part(p), :] = decode(p, me_l, total)
         feat_ref[part(p), :] = feats[p, pl.ds(2 * me_f, 2)].reshape(seq, block)
 
         @pl.when(has_next)
@@ -399,12 +403,7 @@
                 def _():
                     rest = att[part(p), :] - nbuf[p].astype(F32)
                     total = jnp.where(me_l + 1 == t, rest, 0.0)
-                    for s in range(feat_n):
-                        total += lax.dot_general(
-                            features(p, s), wd[t, :, pl.ds(s * block, block)], NT,
-                            preferred_element_type=F32,
-                        )
-                    acc_out[p, t] = total
+                    acc_out[p, t] = decode(p, t, total)
 
                     @pl.when(has_prev)
                     def _():
@@ -502,8 +501,8 @@
         ]
         + [pltpu.VMEM((feat_n, width, block), BF16)] * 3
         + [
-            dma((16,)), dma((1,)), dma((prompts,)), dma((prompts, 2)), dma((prompts, feat_n)), dma((prompts,)),
-            dma((prompts, feat_n)), dma((prompts,)), dma((prompts,)), dma((prompts, layers)),
+            dma((4,)), dma((1,)), dma((prompts,)), dma((prompts, 2)), dma((prompts, feat_n)), dma((prompts,)),
+            dma((prompts, feat_n)), dma((prompts,)), dma((prompts,)), dma((prompts, layers - 1)),
             dma((3, feat_n)), dma((shares, feat_n)),
         ],
         compiler_params=pltpu.CompilerParams(collective_id=0, has_side_effects=True),

time: 58.2 us -> 57.7 us (level)
  no operation moved by 1% of the time
where the time goes in v4:
time: 57.7 us; the launch traced here: 57.5 us
  Pallas kernels  56.2 us (97%)
  between operations  1.29 us (2%)
    pallas_call x1, Pallas kernels, local(): pl.pallas_call(functools.partial(kernel, sizes), out_shape=(pltpu.VMEM((w...  55.5 us

profile of v4, /device:TPU:7, one launch (start us, length us, event | category | flops | bytes accessed | tf_op | source)
XLA Modules:
  0.0 57.5 jit_solution(10914067856057575602)
XLA Ops:
  1.3 55.5 %shard_map.158 = (f32[448,128]{1,0:T(8,128)S(1)}, bf16[128,128]{1,0:T(8,128)(2,1)S(1)}) custom-call(s32[2]{0:T(128)} %lengths_in.1, f32[64]{0:T(128)} %table_in.1, s32[1,1]{1,0:T(1,128)S(6)} %copy.17.chosen_in, f32[1,128]{1,0:T(1,128)} %attn_in.1, f32[1,128]{1,0:T(1,128)} %mlp_in.1, f32[1,128]{1,0:T(1,128)} %bias_in.1, s32[1,4096]{1,0:T(1,128)} %mode_in.1, ...), custom_call_target="tpu_custom_call" | custom-call | tf_op jit(solution)/shard_map/pallas_call | solution.py:477
  56.8 0.7 %shard_map.159 = (f32[448,128]{1,0:T(8,128)}, bf16[128,128]{1,0:T(8,128)(2,1)}) custom-call(f32[448,128]{1,0:T(8,128)S(1)} %get-tuple-element.6.x_ref, bf16[128,128]{1,0:T(8,128)(2,1)S(1)} %get-tuple-element.7.f_ref), custom_call_target="tpu_custom_call" | custom-call | tf_op jit(solution)/shard_map/pallas_call | solution.py:511

commit v5 on v4

--- a/solution.py
+++ b/solution.py
@@ -26,7 +26,7 @@
     x_t, err_t, pat, wv, wo, we, wd,
     xbuf, slots, nbuf, normed, masked, part_v, part_v2, vals, part_e, e_out, e_in, feats,
     acc_in, acc_out, att, err, wek, relay_in, relay_mid,
-    local_sem, sent, up_sent, own_recv, xs_recv, t_recv, v_recv, m_recv, f_recv, a_recv, w_recv, b_recv,
+    local_sem, ready, sent, up_sent, own_recv, xs_recv, t_recv, v_recv, m_recv, f_recv, a_recv, w_recv, b_recv,
 ):
     layers, feat_n, seq, prompts, head_dim, per_group, kv, width, block, rows, entries, shares = sizes
     half = seq // 2
@@ -69,12 +69,10 @@
     for j in range(1, feat_n):
         for t in range(2):
             greet({"feat": (me_f + j) % feat_n, "tok": t})
-    pl.when(has_next)(lambda: greet({"layer": nxt}))
     for s in range(feat_n):
-        pl.when(both(has_prev, jnp.abs(me_f - s) != 1))(lambda: greet({"layer": prv, "feat": s}))
+        pl.when(both(has_next, jnp.abs(me_f - s) != 1))(lambda: greet({"layer": nxt, "feat": s}))
     for g in range(1, shares):
         pl.when(is_first)(lambda: greet({"groups": (me_g + g) % shares, "layer": nxt}))
-        pl.when(me_l == 1)(lambda: greet({"groups": (me_g + g) % shares, "layer": prv}))
     greet({"tok": other})
 
     def send(src, dst, rs, where):
@@ -114,9 +112,14 @@
             slots[p, me_f] = x_half[p * seq : (p + 1) * seq]
             xbuf[p] = x_rows[p * seq : (p + 1) * seq]
 
-    extra = (shares - 1) * (1 - jnp.minimum(me_l // 2, 1))
-    above = jnp.minimum(layers - 1 - me_l, 1) * (feat_n - 2 + jnp.where(at_end, 1, 0))
-    pl.semaphore_wait(barrier, 2 * feat_n - 1 + jnp.minimum(me_l, 1) + above + extra)
+    met = feat_n - 2 + jnp.where(at_end, 1, 0)
+    second = jnp.minimum(me_l, 1) * (1 - jnp.minimum(me_l // 2, 1))
+    pl.semaphore_wait(barrier, 2 * feat_n - 1 + jnp.minimum(me_l, 1) * met + second * (shares - 1))
+    for s in range(feat_n):
+        @pl.when(both(has_prev, jnp.abs(me_f - s) != 1))
+        def _():
+            slot = jnp.minimum(jnp.abs(me_f - s), 1)
+            pl.semaphore_signal(ready.at[slot], inc=1, device_id={"layer": prv, "feat": s}, device_id_type=mesh_id)
 
     def share_x(p, step, cond):
         to = me_f + step
@@ -184,6 +187,7 @@
     def next_to(j):
         return jnp.abs(peer(j) - me_f) == 1
 
+    pl.when(has_next)(lambda: pl.semaphore_wait(ready.at[0], 1))
     for j in range(1, feat_n):
         launch(first_up[j - 1], both(is_first, distant(j)))
     for j in range(1, feat_n):
@@ -368,6 +372,7 @@
     def acc_copy(p, t):
         return send(acc_out.at[p, t], acc_in.at[p, t], a_recv.at[p, t - 1], {"layer": nxt})
 
+    pl.when(has_next)(lambda: pl.semaphore_wait(ready.at[1], met - 1))
     for p in streams:
         @pl.when(has_prev)
         def _():
@@ -501,7 +506,7 @@
         ]
         + [pltpu.VMEM((feat_n, width, block), BF16)] * 3
         + [
-            dma((4,)), dma((1,)), dma((prompts,)), dma((prompts, 2)), dma((prompts, feat_n)), dma((prompts,)),
+            dma((4,)), pltpu.SemaphoreType.REGULAR((2,)), dma((1,)), dma((prompts,)), dma((prompts, 2)), dma((prompts, feat_n)), dma((prompts,)),
             dma((prompts, feat_n)), dma((prompts,)), dma((prompts,)), dma((prompts, layers - 1)),
             dma((3, feat_n)), dma((shares, feat_n)),
         ],

time: 57.7 us -> 57.1 us (0.990)
  no operation moved by 1% of the time
where the time goes in v5:
time: 57.1 us; the launch traced here: 57 us
  Pallas kernels  55.7 us (98%)
  between operations  1.29 us (2%)
    pallas_call x1, Pallas kernels, local(): pl.pallas_call(functools.partial(kernel, sizes), out_shape=(pltpu.VMEM((w...  55 us

profile of v5, /device:TPU:7, one launch (start us, length us, event | category | flops | bytes accessed | tf_op | source)
XLA Modules:
  0.0 57.0 jit_solution(5354327514108720516)
XLA Ops:
  1.3 55.0 %shard_map.158 = (f32[448,128]{1,0:T(8,128)S(1)}, bf16[128,128]{1,0:T(8,128)(2,1)S(1)}) custom-call(s32[2]{0:T(128)} %lengths_in.1, f32[64]{0:T(128)} %table_in.1, s32[1,1]{1,0:T(1,128)S(6)} %copy.17.chosen_in, f32[1,128]{1,0:T(1,128)} %attn_in.1, f32[1,128]{1,0:T(1,128)} %mlp_in.1, f32[1,128]{1,0:T(1,128)} %bias_in.1, s32[1,4096]{1,0:T(1,128)} %mode_in.1, ...), custom_call_target="tpu_custom_call" | custom-call | tf_op jit(solution)/shard_map/pallas_call | solution.py:482
  56.3 0.7 %shard_map.159 = (f32[448,128]{1,0:T(8,128)}, bf16[128,128]{1,0:T(8,128)(2,1)}) custom-call(f32[448,128]{1,0:T(8,128)S(1)} %get-tuple-element.6.x_ref, bf16[128,128]{1,0:T(8,128)(2,1)S(1)} %get-tuple-element.7.f_ref), custom_call_target="tpu_custom_call" | custom-call | tf_op jit(solution)/shard_map/pallas_call | solution.py:516

commit v6 on v5

--- a/solution.py
+++ b/solution.py
@@ -26,7 +26,7 @@
     x_t, err_t, pat, wv, wo, we, wd,
     xbuf, slots, nbuf, normed, masked, part_v, part_v2, vals, part_e, e_out, e_in, feats,
     acc_in, acc_out, att, err, wek, relay_in, relay_mid,
-    local_sem, ready, sent, up_sent, own_recv, xs_recv, t_recv, v_recv, m_recv, f_recv, a_recv, w_recv, b_recv,
+    local_sem, ready, sent, up_sent, own_recv, xs_recv, t_recv, v_recv, vh_recv, m_recv, f_recv, a_recv, w_recv, b_recv,
 ):
     layers, feat_n, seq, prompts, head_dim, per_group, kv, width, block, rows, entries, shares = sizes
     half = seq // 2
@@ -246,9 +246,18 @@
     def arrival(k):
         return jnp.where(at_end, far(feat_n - 1 - k), far(k - 1)) if k else me_f
 
+    def splits(p):
+        return p + 1 < prompts
+
+    def rows_of(p, s, t):
+        return vals.at[p, s, pl.ds(pl.multiple_of(t * half, 16), half)]
+
     def v_sends(p):
-        mine = vals.at[p, me_f]
-        return [send(mine, mine, v_recv.at[p, me_f], {"feat": far(k)}) for k in range(feat_n - 1)]
+        if splits(p):
+            mine, arrive = rows_of(p, me_f, me_t), vh_recv.at[p, me_f, me_t]
+        else:
+            mine, arrive = vals.at[p, me_f], v_recv.at[p, me_f]
+        return [send(mine, mine, arrive, {"feat": far(k)}) for k in range(feat_n - 1)]
 
     def v_finish(p, cond):
         @pl.when(cond)
@@ -308,10 +317,22 @@
         mine = 2 * (feat_n - 1) + other
         return send(e_out.at[p, mine], e_in.at[p, 2 * me_f + me_t], m_recv.at[p], {"tok": other})
 
+    def hand_over(p, s):
+        got, arrive = rows_of(p, s, me_t), vh_recv.at[p, s, me_t]
+        pl.when(me_f != s)(lambda: landed(got, arrive))
+        launch(send(got, got, arrive, {"tok": other}), me_f != s)
+
     for p in streams:
         total = jnp.zeros((seq, width), F32)
-        for s in order:
-            pl.when(me_f != s)(lambda: landed(vals.at[p, s], v_recv.at[p, s]))
+        if splits(p):
+            hand_over(p, order[0])
+        for n, s in enumerate(order):
+            if splits(p):
+                if n + 1 < feat_n:
+                    hand_over(p, order[n + 1])
+                pl.when(me_f != s)(lambda: landed(rows_of(p, s, other), vh_recv.at[p, s, other]))
+            else:
+                pl.when(me_f != s)(lambda: landed(vals.at[p, s], v_recv.at[p, s]))
             group = s * kv // head_dim
             d0 = s * kv % head_dim
             heads = jnp.dot(masked[group, p], vals[p, s], preferred_element_type=F32).astype(BF16)
@@ -507,7 +528,7 @@
         + [pltpu.VMEM((feat_n, width, block), BF16)] * 3
         + [
             dma((4,)), pltpu.SemaphoreType.REGULAR((2,)), dma((1,)), dma((prompts,)), dma((prompts, 2)), dma((prompts, feat_n)), dma((prompts,)),
-            dma((prompts, feat_n)), dma((prompts,)), dma((prompts,)), dma((prompts, layers - 1)),
+            dma((prompts, feat_n)), dma((prompts, feat_n, 2)), dma((prompts,)), dma((prompts,)), dma((prompts, layers - 1)),
             dma((3, feat_n)), dma((shares, feat_n)),
         ],
         compiler_params=pltpu.CompilerParams(collective_id=0, has_side_effects=True),

time: 57.1 us -> 56 us (0.981)
  Pallas kernels: 55.7 us -> 54.5 us
    pallas_call x1, Pallas kernels: 55 us -> 53.8 us  [local(): pl.pallas_call(functools.partial(kernel, sizes), out_shape=(pltpu.VMEM((w...]
where the time goes in v6:
time: 56 us; the launch traced here: 55.8 us
  Pallas kernels  54.5 us (97%)
  between operations  1.29 us (2%)
    pallas_call x1, Pallas kernels, local(): pl.pallas_call(functools.partial(kernel, sizes), out_shape=(pltpu.VMEM((w...  53.8 us

profile of v6, /device:TPU:7, one launch (start us, length us, event | category | flops | bytes accessed | tf_op | source)
XLA Modules:
  0.0 55.8 jit_solution(2791108718295098441)
XLA Ops:
  1.3 53.8 %shard_map.158 = (f32[448,128]{1,0:T(8,128)S(1)}, bf16[128,128]{1,0:T(8,128)(2,1)S(1)}) custom-call(s32[2]{0:T(128)} %lengths_in.1, f32[64]{0:T(128)} %table_in.1, s32[1,1]{1,0:T(1,128)S(6)} %copy.17.chosen_in, f32[1,128]{1,0:T(1,128)} %attn_in.1, f32[1,128]{1,0:T(1,128)} %mlp_in.1, f32[1,128]{1,0:T(1,128)} %bias_in.1, s32[1,4096]{1,0:T(1,128)} %mode_in.1, ...), custom_call_target="tpu_custom_call" | custom-call | tf_op jit(solution)/shard_map/pallas_call | solution.py:503
  55.1 0.7 %shard_map.159 = (f32[448,128]{1,0:T(8,128)}, bf16[128,128]{1,0:T(8,128)(2,1)}) custom-call(f32[448,128]{1,0:T(8,128)S(1)} %get-tuple-element.6.x_ref, bf16[128,128]{1,0:T(8,128)(2,1)S(1)} %get-tuple-element.7.f_ref), custom_call_target="tpu_custom_call" | custom-call | tf_op jit(solution)/shard_map/pallas_call | solution.py:537

commit v7 on v6

--- a/solution.py
+++ b/solution.py
@@ -238,6 +238,10 @@
                 to = me_f + step
                 inside = both(has_prev, both(to >= 0, to < feat_n))
                 launch(send(slot, slot, xs_recv.at[p, me_f], {"feat": jnp.clip(to, 0, feat_n - 1)}), inside)
+            if p == 0:
+                for k in range(feat_n - 1):
+                    onward = both(jnp.abs(far(k) - me_f) > 1, jnp.logical_not(at_end))
+                    launch(send(slot, slot, xs_recv.at[p, me_f], {"feat": far(k)}), both(has_prev, onward))
 
         @pl.when(has_prev)
         def _():
@@ -418,7 +422,7 @@
             to = far(k)
             launch(
                 send(nbuf.at[p], slots.at[p, me_f], xs_recv.at[p, me_f], {"layer": nxt, "feat": to}),
-                both(has_next, jnp.abs(to - me_f) > 1),
+                both(both(has_next, jnp.abs(to - me_f) > 1), at_end if p == 0 else has_next),
             )
 
     @pl.when(has_next)

time: 56 us -> 54.3 us (0.970)
  Pallas kernels: 54.5 us -> 52.9 us
    pallas_call x1, Pallas kernels: 53.8 us -> 52.2 us  [local(): pl.pallas_call(functools.partial(kernel, sizes), out_shape=(pltpu.VMEM((w...]
where the time goes in v7:
time: 54.3 us; the launch traced here: 54.2 us
  Pallas kernels  52.9 us (97%)
  between operations  1.29 us (2%)
    pallas_call x1, Pallas kernels, local(): pl.pallas_call(functools.partial(kernel, sizes), out_shape=(pltpu.VMEM((w...  52.2 us

profile of v7, /device:TPU:7, one launch (start us, length us, event | category | flops | bytes accessed | tf_op | source)
XLA Modules:
  0.0 54.2 jit_solution(16356507937089138227)
XLA Ops:
  1.3 52.2 %shard_map.158 = (f32[448,128]{1,0:T(8,128)S(1)}, bf16[128,128]{1,0:T(8,128)(2,1)S(1)}) custom-call(s32[2]{0:T(128)} %lengths_in.1, f32[64]{0:T(128)} %table_in.1, s32[1,1]{1,0:T(1,128)S(6)} %copy.17.chosen_in, f32[1,128]{1,0:T(1,128)} %attn_in.1, f32[1,128]{1,0:T(1,128)} %mlp_in.1, f32[1,128]{1,0:T(1,128)} %bias_in.1, s32[1,4096]{1,0:T(1,128)} %mode_in.1, ...), custom_call_target="tpu_custom_call" | custom-call | tf_op jit(solution)/shard_map/pallas_call | solution.py:507
  53.5 0.7 %shard_map.159 = (f32[448,128]{1,0:T(8,128)}, bf16[128,128]{1,0:T(8,128)(2,1)}) custom-call(f32[448,128]{1,0:T(8,128)S(1)} %get-tuple-element.6.x_ref, bf16[128,128]{1,0:T(8,128)(2,1)S(1)} %get-tuple-element.7.f_ref), custom_call_target="tpu_custom_call" | custom-call | tf_op jit(solution)/shard_map/pallas_call | solution.py:541
